TPU v7x, 128 devices: a whole 4x4x4 slice. The times are simulated.
128 devices in a mesh: node: 64 (over z, y, x), freq: 2 (over core).
Axes of the slice: x: 4, y: 4, z: 4, core: 2. Of those that a mesh axis runs over, the one named last changes fastest.
Arguments:
- voltage: float32 [128, 1048576], P('freq', 'node'), may hold values from -0.75 to 0.75
- node_cond: float32 [1048576], P('node'), may hold values from 0.5 to 2
- model_table: float32 [6, 64], replicated, may hold values from 0.25 to 1.5
- model_index: int32 [262144], P('node'), may hold values from 0 to 63
- send_nodes: int32 [64, 64, 2, 128], P('node'), may hold values from 0 to 16384, as said below
- term_slot: int32 [4, 262144], P(None, 'node'), may hold values from 0 to 8191, as said below
Outputs:
- residual: float32 [128, 1048576], P('freq', 'node')
Inputs may be any that keep to these rules, and one draw needn't show every extreme that they name: Each list send_nodes[s, d, g] names local node indices of node group s (0 to 16383) in its first entries and 16384, an empty slot, in the rest; every list has at least one node and the lists of a node group to itself are full. `term_slot`: entry s * 128 + j names row j of the list that node group s sends to the transistor's own node group and transistor group; that row is never empty.
All inputs are finite; a program needn't handle non-finite values.
Results may differ from a plain program's by a relative error of at most 0.000064.
Values sent between devices are 32-bit elements; how exact they have to be, the bound alone decides.
No kernel may reach another device: no remote copies, remote signals or barrier semaphores. Data moves between devices by JAX's collectives and lax.ppermute only.
A program may use at most 128 MiB of HBM per device.

v0:
```python
import jax
import jax.numpy as jnp
from jax import lax
from jax.sharding import PartitionSpec as P

OMEGA = 0.05
HIGH = lax.Precision.HIGHEST


def dft_tables(npoints):
    half_len = npoints // 2
    time_idx = jnp.arange(npoints, dtype=jnp.int32)[:, None]
    row_idx = jnp.arange(npoints, dtype=jnp.int32)[None, :]
    is_sine = (row_idx >= half_len) & (row_idx < npoints - 1)
    edge_row = (row_idx == 0) | (row_idx == npoints - 1)
    harmonic = jnp.where(
        row_idx < half_len,
        row_idx,
        jnp.where(row_idx == npoints - 1, half_len, row_idx - half_len + 1),
    )
    phases = 2.0 * jnp.pi / npoints * (time_idx * harmonic % npoints).astype(jnp.float32)
    basis_rows = jnp.where(is_sine, jnp.sin(phases), jnp.cos(phases))
    weight = jnp.where(edge_row, 1.0 / npoints, 2.0 / npoints).astype(jnp.float32)
    deriv_rate = OMEGA * harmonic.astype(jnp.float32) * weight
    slope_rows = jnp.where(
        is_sine,
        -deriv_rate * jnp.cos(phases),
        jnp.where(edge_row, 0.0, deriv_rate * jnp.sin(phases)),
    )
    return (basis_rows, (weight * basis_rows).T, slope_rows.T)


def soft_bend(values):
    return values + 0.5 * jnp.tanh(values)


def compact_model(term_volts, params):
    drain_v = term_volts[:, 0]
    gate_v = term_volts[:, 1]
    source_v = term_volts[:, 2]
    bulk_v = term_volts[:, 3]
    pinch_v = (gate_v - params[0]) / (1.0 + params[2])
    forward = jnp.square(jax.nn.softplus(0.5 * (pinch_v - source_v)))
    reverse = jnp.square(jax.nn.softplus(0.5 * (pinch_v - drain_v)))
    channel = params[1] * (forward - reverse)
    quiet = jnp.zeros_like(channel)
    current = jnp.stack([channel, quiet, -channel, quiet], axis=1)
    gate_src = params[3] * soft_bend(gate_v - source_v)
    gate_drn = params[4] * soft_bend(gate_v - drain_v)
    drain_blk = params[5] * soft_bend(drain_v - bulk_v)
    charge = jnp.stack([drain_blk - gate_drn, gate_src + gate_drn, -gate_src, -drain_blk], axis=1)
    return (current, charge)


def model_params(table, indices):
    onehot = (jnp.arange(table.shape[1], dtype=jnp.int32)[:, None] == indices[None, :]).astype(
        jnp.float32
    )
    return jnp.dot(table, onehot, precision=HIGH)


def per_device(voltage, node_cond, model_table, model_index, send_nodes, term_slot):
    harm_rows = voltage.shape[0]
    peer_count = send_nodes.shape[1]
    groups = send_nodes.shape[2]
    slot_count = send_nodes.shape[3]
    tr_dev = term_slot.shape[1]
    tr_local = tr_dev // groups
    tables = dft_tables(harm_rows * groups)
    synthesis, analysis, slope_table = tables
    send_list = send_nodes.reshape(-1)
    volt_rows = voltage.T
    picked_rows = jnp.take(volt_rows, send_list, axis=0, mode="fill", fill_value=0.0)
    outgoing = picked_rows.T.reshape(harm_rows, peer_count, groups, slot_count)
    start = lax.axis_index("freq") * tr_local
    params = model_params(model_table, lax.dynamic_slice_in_dim(model_index, start, tr_local))
    source_dev = term_slot // slot_count
    slot_pos = term_slot % slot_count
    group_pos = jnp.arange(tr_dev, dtype=jnp.int32) // tr_local
    flat_index = ((source_dev * groups + group_pos[None, :]) * slot_count + slot_pos).reshape(-1)
    arrived = lax.all_to_all(outgoing, "node", split_axis=1, concat_axis=1, tiled=True)
    arrived_rows = arrived.reshape(harm_rows, -1).T
    term_volts = jnp.take(arrived_rows, flat_index, axis=0).T.reshape(harm_rows, 4, tr_dev)
    spectra = lax.all_to_all(term_volts, "freq", split_axis=2, concat_axis=0, tiled=True)
    waveforms = jnp.einsum("th,hkn->tkn", synthesis, spectra, precision=HIGH)
    current, charge = compact_model(waveforms, params)
    amplitudes = jnp.einsum("ht,tkn->hkn", analysis, current, precision=HIGH) + jnp.einsum(
        "ht,tkn->hkn", slope_table, charge, precision=HIGH
    )
    returned = lax.all_to_all(amplitudes, "freq", split_axis=0, concat_axis=2, tiled=True)
    back_rows = returned.reshape(harm_rows, -1).T
    slot_rows = (
        jnp.zeros((peer_count * groups * slot_count, harm_rows), jnp.float32)
        .at[flat_index]
        .add(back_rows)
    )
    incoming = lax.all_to_all(
        slot_rows.T.reshape(harm_rows, peer_count, groups, slot_count),
        "node",
        split_axis=1,
        concat_axis=1,
        tiled=True,
    )
    residual_rows = node_cond[:, None] * volt_rows
    residual_rows = residual_rows.at[send_list].add(incoming.reshape(harm_rows, -1).T, mode="drop")
    return residual_rows.T


def solution(mesh):
    return jax.shard_map(
        per_device,
        mesh=mesh,
        in_specs=(
            P("freq", "node"),
            P("node"),
            P(),
            P("node"),
            P("node", None, None, None),
            P(None, "node"),
        ),
        out_specs=P("freq", "node"),
        check_vma=False,
    )
```

profile of v0, /device:TPU:1, one launch (start us, length us, event | category | flops | bytes accessed | tf_op | source)
XLA Modules:
  0.0 624.6 jit_solution(14205715701475163053)
XLA Ops:
  0.0 6.9 %copy.28 = f32[64,16384]{0,1:T(8,128)} copy(f32[64,16384]{1,0:T(8,128)} %param.6) | data formatting | bytes 8388608 | tf_op args[0]
  7.1 57.9 %gather_fusion = f32[16384,64]{1,0:T(8,128)} fusion(f32[16384,64]{1,0:T(8,128)} %bitcast.60, s32[16384]{0:T(1024)S(1)} %broadcast_clamp_fusion.1), kind=kCustom, calls=%fused_computation | custom fusion | bytes 8454144 | tf_op jit(solution)/shard_map/jit(_take)/gather | solution.py:73
  64.9 13.1 %broadcast_select_fusion.1 = f32[16384,64]{1,0:T(8,128)} fusion(f32[16384,64]{1,0:T(8,128)} %gather_fusion, pred[16384]{0:T(1024)(128)(4,1)S(1)} %compare_and_fusion), kind=kLoop, calls=%fused_computation.23 | loop fusion | flops 1048576 | bytes 8404992 | tf_op jit(solution)/shard_map/jit(_take)/select_n | solution.py:73
  84.8 12.5 %all-to-all-start = ((f32[64,64,2,128]{3,0,2,1:T(8,128)}), f32[64,64,2,128]{3,0,2,1:T(8,128)}, u32[]{:S(2)}, u32[]{:S(2)}) async-start(f32[64,64,2,128]{3,0,2,1:T(8,128)} %copy.29), calls=%async_computation | async-start | bytes 8388608 | tf_op jit(solution)/shard_map/all_to_all | solution.py:81
  98.3 52.1 %all-to-all-done = f32[64,64,2,128]{3,0,2,1:T(8,128)} async-done(((f32[64,64,2,128]{3,0,2,1:T(8,128)}), f32[64,64,2,128]{3,0,2,1:T(8,128)}, u32[]{:S(2)}, u32[]{:S(2)}) %all-to-all-start) | async-done | bytes 4194336 | tf_op jit(solution)/shard_map/all_to_all | solution.py:81
  150.3 6.9 %copy.30 = f32[64,64,2,128]{0,3,2,1:T(8,128)} copy(f32[64,64,2,128]{3,0,2,1:T(8,128)} %all-to-all-done) | data formatting | bytes 8388608 | tf_op jit(solution)/shard_map/all_to_all | solution.py:81
  157.2 57.9 %gather_fusion.1 = f32[16384,64]{1,0:T(8,128)} fusion(f32[16384,64]{1,0:T(8,128)} %bitcast.61, s32[16384]{0:T(1024)S(1)} %broadcast_clamp_fusion), kind=kCustom, calls=%fused_computation.1 | custom fusion | bytes 8454144 | tf_op jit(solution)/shard_map/jit(_take)/gather | solution.py:83
  215.1 11.8 %broadcast_select_fusion = f32[16384,64]{1,0:T(8,128)S(1)} fusion(f32[16384,64]{1,0:T(8,128)} %gather_fusion.1, pred[16384]{0:T(1024)(128)(4,1)S(1)} %compare_and_fusion.1), kind=kLoop, calls=%fused_computation.20 | loop fusion | flops 1048576 | bytes 8404992 | tf_op jit(solution)/shard_map/jit(_take)/select_n | solution.py:83
  226.8 18.6 %copy.47 = f32[64,4,4096]{0,1,2:T(4,128)} copy(f32[64,4,4096]{0,2,1:T(8,128)S(1)} %bitcast.64) | data formatting | bytes 8388608 | tf_op jit(solution)/shard_map/reshape | solution.py:83
  245.5 11.2 %reshape.282 = f32[2,1,524288]{2,1,0:T(1,128)} reshape(f32[4096,4,64]{2,1,0:T(4,128)} %bitcast.67) | data formatting | bytes 8388608
  256.7 14.5 %all_to_all.43 = f32[2,1,524288]{2,1,0:T(1,128)} all-to-all(f32[2,1,524288]{2,1,0:T(1,128)} %reshape.282), channel_id=1, replica_groups=mesh['node'=64,'freq'=2] {'freq'}, dimensions={0} | all-to-all | bytes 8388608 | tf_op jit(solution)/shard_map/all_to_all | solution.py:84
  271.6 17.4 %reduce = f32[2,524288]{1,0:T(2,128)} reduce(f32[2,1,524288]{2,1,0:T(1,128)} %all_to_all.43, f32[]{:T(128)} %broadcast.396), dimensions={1}, to_apply=%all_to_all.31.reduce_sub_computation | reduce | bytes 8388612 | tf_op jit(solution)/shard_map/all_to_all | solution.py:84
  289.0 12.2 %reshape.283 = f32[4096,4,64]{2,1,0:T(4,128)} reshape(f32[2,524288]{1,0:T(2,128)} %reduce) | data formatting | bytes 8388608
  301.3 12.6 %copy.43 = f32[64,4,2,2048]{3,2,0,1:T(2,128)} copy(f32[64,4,2,2048]{0,1,3,2:T(4,128)} %bitcast.65) | data formatting | bytes 8388608 | tf_op jit(solution)/shard_map/all_to_all | solution.py:84
  336.5 8.2 %all_to_all.44 = f32[128,4,2048]{2,1,0:T(4,128)} all-to-all(f32[128,4,2048]{2,1,0:T(4,128)S(1)} %copy.35), channel_id=1, replica_groups=mesh['node'=64,'freq'=2] {'freq'}, dimensions={0} | all-to-all | bytes 8388608 | tf_op jit(solution)/shard_map/all_to_all | solution.py:90
  344.7 7.5 %copy.36 = f32[64,4,2,2048]{0,3,2,1:T(8,128)} copy(f32[64,4,2,2048]{3,1,0,2:T(4,128)} %bitcast.69) | data formatting | bytes 8388608 | tf_op jit(solution)/shard_map/all_to_all | solution.py:90
  352.2 91.3 %scatter_custom_fusion = f32[16384,64]{1,0:T(8,128)} fusion(s32[16384]{0:T(1024)S(1)} %bitcast.79, f32[16384,64]{1,0:T(8,128)} %bitcast.72, f32[]{:T(128)} %constant.97.clone.1), kind=kCustom, calls=%fused_computation.21 | custom fusion | flops 1048576 | bytes 4194816 | tf_op jit(solution)/shard_map/scatter-add | solution.py:95
  450.3 7.8 %all-to-all-start.3 = ((f32[64,64,2,128]{3,0,2,1:T(8,128)}), f32[64,64,2,128]{3,0,2,1:T(8,128)}, u32[]{:S(2)}, u32[]{:S(2)}) async-start(f32[64,64,2,128]{3,0,2,1:T(8,128)} %copy.37), calls=%async_computation.3 | async-start | bytes 8388608 | tf_op jit(solution)/shard_map/all_to_all | solution.py:97
  458.1 7.9 %broadcast_multiply_fusion = f32[16384,64]{1,0:T(8,128)} fusion(f32[16384]{0:T(1024)S(1)} %copy-done.4, f32[64,16384]{0,1:T(8,128)} %copy.28), kind=kLoop, calls=%fused_computation.24 | loop fusion | flops 1048576 | bytes 8454144 | tf_op jit(solution)/shard_map/mul | solution.py:104
  466.0 45.6 %all-to-all-done.3 = f32[64,64,2,128]{3,0,2,1:T(8,128)} async-done(((f32[64,64,2,128]{3,0,2,1:T(8,128)}), f32[64,64,2,128]{3,0,2,1:T(8,128)}, u32[]{:S(2)}, u32[]{:S(2)}) %all-to-all-start.3) | async-done | bytes 4194336 | tf_op jit(solution)/shard_map/all_to_all | solution.py:97
  511.5 7.4 %copy.38 = f32[64,64,2,128]{3,2,1,0:T(2,128)} copy(f32[64,64,2,128]{3,0,2,1:T(8,128)} %all-to-all-done.3) | data formatting | bytes 8388608 | tf_op jit(solution)/shard_map/all_to_all | solution.py:97
  525.4 6.9 %copy.39 = f32[16384,64]{1,0:T(8,128)} copy(f32[16384,64]{0,1:T(8,128)} %bitcast.70) | data formatting | bytes 8388608 | tf_op jit(solution)/shard_map/transpose | solution.py:105
  532.3 85.3 %scatter_fusion = f32[16384,64]{1,0:T(8,128)} fusion(f32[16384,64]{1,0:T(8,128)} %broadcast_multiply_fusion, s32[16384]{0:T(1024)S(1)} %bitcast.74, f32[16384,64]{1,0:T(8,128)} %copy.39), kind=kCustom, calls=%fused_computation.3 | custom fusion | flops 1048576 | bytes 12648448 | tf_op jit(solution)/shard_map/scatter-add | solution.py:105
  617.6 6.8 %copy.40 = f32[64,16384]{1,0:T(8,128)} copy(f32[64,16384]{0,1:T(8,128)} %bitcast.62) | data formatting | bytes 8388608 | tf_op jit(solution)/shard_map/transpose | solution.py:106
  (41 shorter events, 44.0 us)
Async XLA Ops:
  0.0 97.7 %copy-start = (f32[6,64]{1,0:T(8,128)S(1)}, f32[6,64]{1,0:T(8,128)}, u32[]{:S(2)}) copy-start(f32[6,64]{1,0:T(8,128)} %param.8) | copy-start | bytes 4612
  0.0 6.9 %copy-start.2 = (s32[1,64,2,128]{3,2,1,0:T(2,128)S(1)}, s32[1,64,2,128]{3,2,1,0:T(2,128)}, u32[]{:S(2)}) copy-start(s32[1,64,2,128]{3,2,1,0:T(2,128)} %param.10) | copy-start | bytes 196612
  84.8 12.6 %copy-start.3 = (s32[4,4096]{1,0:T(4,128)S(1)}, s32[4,4096]{1,0:T(4,128)}, u32[]{:S(2)}) copy-start(s32[4,4096]{1,0:T(4,128)} %param.11) | copy-start | bytes 196612
  84.8 12.9 %copy-start.5 = (s32[4096]{0:T(1024)S(1)}, s32[4096]{0:T(1024)}, u32[]{:S(2)}) copy-start(s32[4096]{0:T(1024)} %param.9) | copy-start | bytes 49156
  84.8 65.5 %all-to-all-start = ((f32[64,64,2,128]{3,0,2,1:T(8,128)}), f32[64,64,2,128]{3,0,2,1:T(8,128)}, u32[]{:S(2)}, u32[]{:S(2)}) async-start(f32[64,64,2,128]{3,0,2,1:T(8,128)} %copy.29), calls=%async_computation | async-start | bytes 8388608 | tf_op jit(solution)/shard_map/all_to_all | solution.py:81
  450.3 7.8 %copy-start.4 = (f32[16384]{0:T(1024)S(1)}, f32[16384]{0:T(1024)}, u32[]{:S(2)}) copy-start(f32[16384]{0:T(1024)} %param.7) | copy-start | bytes 196612
  450.3 61.3 %all-to-all-start.3 = ((f32[64,64,2,128]{3,0,2,1:T(8,128)}), f32[64,64,2,128]{3,0,2,1:T(8,128)}, u32[]{:S(2)}, u32[]{:S(2)}) async-start(f32[64,64,2,128]{3,0,2,1:T(8,128)} %copy.37), calls=%async_computation.3 | async-start | bytes 8388608 | tf_op jit(solution)/shard_map/all_to_all | solution.py:97
  617.6 6.8 %copy-start.1 = (f32[6,64]{1,0:T(8,128)S(1)}, f32[6,64]{1,0:T(8,128)}, u32[]{:S(2)}) copy-start(f32[6,64]{1,0:T(8,128)} %param.8) | copy-start | bytes 4612
where the time goes:
time: 630 us; the launch traced here: 625 us
  local copies, waits for them, and re-layouts  241 us (38%)
  other arithmetic  229 us (36%)
  waiting for transfers between devices  97.6 us (15%)
  blocking collectives  22.7 us (4%)
  starting transfers between devices  20.3 us (3%)
  matrix products  13.4 us (2%)
    scatter-add x1, other arithmetic, per_device(): slot_rows = jnp.zeros((peer_count * groups * slot_count, harm_rows), jnp....  91.3 us
    scatter-add x1, other arithmetic, per_device(): residual_rows.at[send_list]  85.3 us
    gather x1, local copies, waits for them, and re-layouts, per_device(): jnp.take(arrived_rows, flat_index, axis=0).T.reshape(harm_rows, 4, tr_dev)  57.9 us
    gather x1, local copies, waits for them, and re-layouts, per_device(): jnp.take(volt_rows, send_list, axis=0, mode='fill', fill_value=0.0)  57.9 us
    all_to_all x1, waiting for transfers between devices, per_device(): lax.all_to_all(outgoing, 'node', split_axis=1, concat_axis=1, tiled=True)  52.1 us
    all_to_all x1, waiting for transfers between devices, per_device(): lax.all_to_all(slot_rows.T.reshape(harm_rows, peer_count, groups, slot_co...  45.6 us
    unnamed x17, local copies, waits for them, and re-layouts  30.5 us
    reshape x1, local copies, waits for them, and re-layouts, per_device(): jnp.take(arrived_rows, flat_index, axis=0).T.reshape(harm_rows, 4, tr_dev)  18.6 us
  transfers between devices with their start and end apart: 2, of which 2 were waited for; matrix products, arithmetic and copies ran while one was open for 1% of the time, Pallas kernels for 0%

commit v1 on v0

v1 whole, which is shorter than its diff:
```python
import jax
import jax.numpy as jnp
import numpy as np
from jax import lax
from jax.experimental import pallas as pl
from jax.experimental.pallas import tpu as pltpu
from jax.sharding import PartitionSpec as P

OMEGA = 0.05
HIGH = lax.Precision.HIGHEST
F32 = jnp.float32
BF16 = jnp.bfloat16


def dft_tables(npoints):
    half_len = npoints // 2
    time_idx = np.arange(npoints)[:, None]
    row_idx = np.arange(npoints)[None, :]
    is_sine = (row_idx >= half_len) & (row_idx < npoints - 1)
    edge_row = (row_idx == 0) | (row_idx == npoints - 1)
    harmonic = np.where(row_idx < half_len, row_idx, np.where(row_idx == npoints - 1, half_len, row_idx - half_len + 1))
    phases = 2.0 * np.pi / npoints * (time_idx * harmonic % npoints)
    basis_rows = np.where(is_sine, np.sin(phases), np.cos(phases))
    weight = np.where(edge_row, 1.0 / npoints, 2.0 / npoints)
    deriv_rate = OMEGA * harmonic * weight
    slope_rows = np.where(is_sine, -deriv_rate * np.cos(phases), np.where(edge_row, 0.0, deriv_rate * np.sin(phases)))
    return basis_rows, (weight * basis_rows).T, slope_rows.T


def split_weights(w):
    w = w.astype(np.float32)
    hi = w.astype(jnp.bfloat16)
    lo = (w - hi.astype(np.float32)).astype(jnp.bfloat16)
    return jnp.asarray(hi), jnp.asarray(lo)


def dot3(x, w_hi, w_lo):
    x_hi = x.astype(BF16)
    x_lo = (x - x_hi.astype(F32)).astype(BF16)
    out = jnp.dot(x_hi, w_hi, preferred_element_type=F32)
    out = out + jnp.dot(x_hi, w_lo, preferred_element_type=F32)
    return out + jnp.dot(x_lo, w_hi, preferred_element_type=F32)


def soft_bend(values):
    return values + 0.5 * jnp.tanh(values)


def softplus(x):
    return jnp.maximum(x, 0.0) + jnp.log1p(jnp.exp(-jnp.abs(x)))


def pick_kernel(rows, slots, idx, v_hbm, out_hbm, vbuf, table, obuf, in_sem, out_sem):
    nodes = vbuf.shape[1]
    n_in = in_sem.shape[0]
    n_out = out_sem.shape[0]
    width = nodes // n_in
    half = slots // 2
    peers = obuf.shape[0] // half
    per_out = peers // n_out

    def fetch(c):
        cols = pl.ds(c * width, width)
        return pltpu.make_async_copy(v_hbm.at[:, cols], vbuf.at[:, cols], in_sem.at[c])

    def ship(c):
        part = pl.ds(c * per_out * half, per_out * half)
        return pltpu.make_async_copy(obuf.at[part], out_hbm.at[part], out_sem.at[c])

    for c in range(n_in):
        fetch(c).start()
    table[pl.ds(nodes, 8), :] = jnp.zeros((8, 128), F32)
    for c in range(n_in):
        fetch(c).wait()

        def turn(b, carry, c=c):
            at = pl.multiple_of(c * width + b * 128, 128)
            x = vbuf[:, pl.ds(at, 128)]
            table[pl.ds(at, 128), :] = jnp.concatenate([x, x], axis=0).T
            return carry

        lax.fori_loop(0, width // 128, turn, 0)
    low = lax.broadcasted_iota(jnp.int32, (1, 128), 1) < rows

    def group(c, carry):
        def peer(q, carry):
            p = c * per_out + q
            for j in range(half):
                a = idx[p * slots + j]
                b = idx[p * slots + half + j]
                obuf[pl.ds(p * half + j, 1), :] = jnp.where(low, table[pl.ds(a, 1), :], table[pl.ds(b, 1), :])
            return carry

        lax.fori_loop(0, per_out, peer, 0)
        ship(c).start()
        return carry

    lax.fori_loop(0, n_out, group, 0)
    for c in range(n_out):
        ship(c).wait()


def device_kernel(
    idx, params, syn_hi, syn_lo, ana_hi, ana_lo, x_hbm, out_hbm,
    xbuf, wave, gbuf, qbuf, abuf, acc0, acc1, acc2, acc3, in_sem, out_sem,
):
    accs = (acc0, acc1, acc2, acc3)
    senders, _, half, lanes = xbuf.shape
    n_in = in_sem.shape[0]
    n_out = out_sem.shape[0]
    per_in = senders // n_in
    per_out = senders // n_out
    tr_local = params.shape[0]
    chunk = gbuf.shape[1]
    sub = 64

    def fetch(c):
        part = pl.ds(c * per_in, per_in)
        return pltpu.make_async_copy(x_hbm.at[part], xbuf.at[part], in_sem.at[c])

    def ship(c):
        part = pl.ds(c * per_out, per_out)
        return pltpu.make_async_copy(xbuf.at[part], out_hbm.at[part], out_sem.at[c])

    for c in range(n_in):
        fetch(c).start()

    def clear(i, carry):
        for acc in accs:
            acc[pl.ds(pl.multiple_of(i * 256, 256), 256), :] = jnp.zeros((256, lanes), F32)
        return carry

    lax.fori_loop(0, acc0.shape[0] // 256, clear, 0)

    def synth(c, carry):
        fetch(c).wait()
        x = xbuf[pl.ds(c * per_in, per_in)]
        xx = jnp.concatenate(
            [x[:, 0].reshape(per_in * half, lanes), x[:, 1].reshape(per_in * half, lanes)], axis=1
        )
        y = dot3(xx, syn_hi[...], syn_lo[...])
        for s in range(per_in):
            at = pl.multiple_of((c * per_in + s) * 2 * half, 2 * half)
            wave[pl.ds(at, half), :] = y[s * half : (s + 1) * half, :lanes]
            wave[pl.ds(at + half, half), :] = y[s * half : (s + 1) * half, lanes:]
        return carry

    lax.fori_loop(0, n_in, synth, 0)

    def block(c, carry):
        base = c * chunk

        def collect(i, carry):
            t = i * 16
            for u in range(16):
                for k in range(4):
                    gbuf[k, pl.ds(t + u, 1), :] = wave[pl.ds(idx[k * tr_local + base + t + u], 1), :]
            return carry

        lax.fori_loop(0, chunk // 16, collect, 0)

        def model(i, carry):
            at = pl.ds(pl.multiple_of(i * sub, sub), sub)
            par = params[pl.ds(pl.multiple_of(base + i * sub, sub), sub), :]
            thresh, strength, inv_slope, cap_gs, cap_gd, cap_db = (par[:, m : m + 1] for m in range(6))
            drain, gate, source, bulk = (gbuf[k, at, :] for k in range(4))
            pinch = (gate - thresh) * inv_slope
            forward = softplus(0.5 * (pinch - source))
            reverse = softplus(0.5 * (pinch - drain))
            qbuf[at, 0:lanes] = strength * (forward * forward - reverse * reverse)
            qbuf[at, lanes : 2 * lanes] = cap_gs * soft_bend(gate - source)
            qbuf[at, 2 * lanes : 3 * lanes] = cap_gd * soft_bend(gate - drain)
            qbuf[at, 3 * lanes : 4 * lanes] = cap_db * soft_bend(drain - bulk)
            return carry

        lax.fori_loop(0, chunk // sub, model, 0)
        left = dot3(qbuf[:, : 2 * lanes], ana_hi[:, : 2 * lanes], ana_lo[:, : 2 * lanes])
        right = dot3(qbuf[:, 2 * lanes :], ana_hi[:, 2 * lanes :], ana_lo[:, 2 * lanes :])
        chan, gs = left[:, :lanes], left[:, lanes:]
        gd, db = right[:, :lanes], right[:, lanes:]
        abuf[0] = chan + (db - gd)
        abuf[1] = gs + gd
        abuf[2] = -chan - gs
        abuf[3] = -db

        def spread(i, carry):
            t = i * 8
            for u in range(8):
                for k in range(4):
                    row = pl.ds(idx[k * tr_local + base + t + u], 1)
                    accs[k][row, :] = accs[k][row, :] + abuf[k, pl.ds(t + u, 1), :]
            return carry

        lax.fori_loop(0, chunk // 8, spread, 0)
        return carry

    lax.fori_loop(0, tr_local // chunk, block, 0)
    low = lax.broadcasted_iota(jnp.int32, (half, lanes), 1) < half

    def pack(c, carry):
        for s in range(per_out):
            peer = c * per_out + s
            at = pl.multiple_of(peer * 2 * half, 2 * half)
            first = sum(acc[pl.ds(at, half), :] for acc in accs)
            second = sum(acc[pl.ds(at + half, half), :] for acc in accs)
            xbuf[peer, 0] = jnp.where(low, first, pltpu.roll(second, half, 1))
            xbuf[peer, 1] = jnp.where(low, pltpu.roll(first, half, 1), second)
        ship(c).start()
        return carry

    lax.fori_loop(0, n_out, pack, 0)
    for c in range(n_out):
        ship(c).wait()


def residual_kernel(
    rows, slots, idx, cond, x_hbm, v_hbm, out_hbm,
    xbuf, vbuf, low0, low1, high0, high1, in_sem, v_sem, out_sem,
):
    nodes = vbuf.shape[1]
    half = slots // 2
    n_in = in_sem.shape[0]
    n_out = out_sem.shape[0]
    width = nodes // n_out
    peers = xbuf.shape[0] // half
    per_in = peers // n_in

    def fetch(c):
        part = pl.ds(c * per_in * half, per_in * half)
        return pltpu.make_async_copy(x_hbm.at[part], xbuf.at[part], in_sem.at[c])

    def ship(c):
        cols = pl.ds(c * width, width)
        return pltpu.make_async_copy(vbuf.at[:, cols], out_hbm.at[:, cols], out_sem.at[c])

    v_copy = pltpu.make_async_copy(v_hbm, vbuf, v_sem)
    for c in range(n_in):
        fetch(c).start()
    v_copy.start()

    def clear(i, carry):
        for acc in (low0, low1, high0, high1):
            acc[pl.ds(pl.multiple_of(i * 256, 256), 256), :] = jnp.zeros((256, 128), F32)
        return carry

    lax.fori_loop(0, nodes // 256, clear, 0)

    def group(c, carry):
        fetch(c).wait()

        def peer(q, carry):
            p = c * per_in + q
            for j in range(half):
                acc_a, acc_b = ((low0, high0), (low1, high1))[j % 2]
                x = xbuf[pl.ds(p * half + j, 1), :]
                a = pl.ds(idx[p * slots + j], 1)
                b = pl.ds(idx[p * slots + half + j], 1)
                acc_a[a, :] = acc_a[a, :] + x
                acc_b[b, :] = acc_b[b, :] + x
            return carry

        lax.fori_loop(0, per_in, peer, 0)
        return carry

    lax.fori_loop(0, n_in, group, 0)
    v_copy.wait()
    low = lax.broadcasted_iota(jnp.int32, (128, 128), 1) < rows

    def finish(c, carry):
        def turn(b, carry):
            at = pl.multiple_of(c * width + b * 128, 128)
            part = pl.ds(at, 128)
            both = jnp.where(low, low0[part, :] + low1[part, :], high0[part, :] + high1[part, :]).T
            cols = pl.ds(at, 128)
            vbuf[:, cols] = vbuf[:, cols] * cond[:, cols] + (both[:rows] + both[rows:])
            return carry

        lax.fori_loop(0, width // 128, turn, 0)
        ship(c).start()
        return carry

    lax.fori_loop(0, n_out, finish, 0)
    for c in range(n_out):
        ship(c).wait()


SMEM = pl.BlockSpec(memory_space=pltpu.SMEM)
VMEM = pl.BlockSpec(memory_space=pltpu.VMEM)
ANY = pl.BlockSpec(memory_space=pl.ANY)
ROOM = pltpu.CompilerParams(vmem_limit_bytes=60 * 2**20)


def per_device(voltage, node_cond, model_table, model_index, send_nodes, term_slot):
    rows, nodes = voltage.shape
    senders = send_nodes.shape[1]
    groups = send_nodes.shape[2]
    slots = send_nodes.shape[3]
    half = slots // 2
    peers = senders * groups
    lanes = rows * groups
    tr_local = term_slot.shape[1] // groups
    send_list = send_nodes.reshape(-1)

    outgoing = pl.pallas_call(
        lambda *refs: pick_kernel(rows, slots, *refs),
        out_shape=jax.ShapeDtypeStruct((peers * half, lanes), F32),
        in_specs=[SMEM, ANY],
        out_specs=ANY,
        scratch_shapes=[
            pltpu.VMEM((rows, nodes), F32),
            pltpu.VMEM((nodes + 8, lanes), F32),
            pltpu.VMEM((peers * half, lanes), F32),
            pltpu.SemaphoreType.DMA((8,)),
            pltpu.SemaphoreType.DMA((8,)),
        ],
        compiler_params=ROOM,
        name="pick",
    )(send_list, voltage)

    arrived = lax.all_to_all(outgoing.reshape(peers, half, lanes), ("node", "freq"), 0, 0, tiled=True)

    start = lax.axis_index("freq") * tr_local
    index = lax.dynamic_slice_in_dim(model_index, start, tr_local)
    slot_list = lax.dynamic_slice_in_dim(term_slot, start, tr_local, axis=1).reshape(-1)
    cards = jnp.concatenate([model_table[:2], 1.0 / (1.0 + model_table[2:3]), model_table[3:]], axis=0)
    onehot = (index[:, None] == jnp.arange(cards.shape[1], dtype=jnp.int32)[None, :]).astype(F32)
    params = jnp.dot(onehot, cards.T, precision=HIGH)

    synthesis, analysis, slope_table = dft_tables(lanes)
    syn = np.zeros((2, 2, rows, 2, lanes))
    for f in range(2):
        for q in range(2):
            syn[f, q, :, q, :] = synthesis.T[f * rows : (f + 1) * rows]
    none = np.zeros((lanes, lanes))
    ana = np.concatenate(
        [np.block([[analysis.T, none], [none, slope_table.T]]), np.block([[slope_table.T, none], [none, slope_table.T]])],
        axis=1,
    )
    syn_hi, syn_lo = split_weights(syn.reshape(2 * lanes, 2 * lanes))
    ana_hi, ana_lo = split_weights(ana)
    chunk = 256

    returned = pl.pallas_call(
        device_kernel,
        out_shape=jax.ShapeDtypeStruct((senders, 2, half, lanes), F32),
        in_specs=[SMEM, VMEM, VMEM, VMEM, VMEM, VMEM, ANY],
        out_specs=ANY,
        scratch_shapes=[
            pltpu.VMEM((senders, 2, half, lanes), F32),
            pltpu.VMEM((senders * slots, lanes), F32),
            pltpu.VMEM((4, chunk, lanes), F32),
            pltpu.VMEM((chunk, 4 * lanes), F32),
            pltpu.VMEM((4, chunk, lanes), F32),
        ]
        + [pltpu.VMEM((senders * slots, lanes), F32)] * 4
        + [pltpu.SemaphoreType.DMA((8,)), pltpu.SemaphoreType.DMA((8,))],
        compiler_params=ROOM,
        name="devices",
    )(slot_list, params, syn_hi, syn_lo, ana_hi, ana_lo, arrived.reshape(senders, 2, half, lanes))

    incoming = lax.all_to_all(returned.reshape(peers, half, lanes), ("node", "freq"), 0, 0, tiled=True)

    return pl.pallas_call(
        lambda *refs: residual_kernel(rows, slots, *refs),
        out_shape=jax.ShapeDtypeStruct((rows, nodes), F32),
        in_specs=[SMEM, VMEM, ANY, ANY],
        out_specs=ANY,
        scratch_shapes=[pltpu.VMEM((peers * half, lanes), F32), pltpu.VMEM((rows, nodes), F32)]
        + [pltpu.VMEM((nodes + 8, lanes), F32)] * 4
        + [pltpu.SemaphoreType.DMA((8,)), pltpu.SemaphoreType.DMA, pltpu.SemaphoreType.DMA((8,))],
        compiler_params=ROOM,
        name="residual",
    )(send_list, node_cond.reshape(1, nodes), incoming.reshape(peers * half, lanes), voltage)


def solution(mesh):
    return jax.shard_map(
        per_device,
        mesh=mesh,
        in_specs=(
            P("freq", "node"),
            P("node"),
            P(),
            P("node"),
            P("node", None, None, None),
            P(None, "node"),
        ),
        out_specs=P("freq", "node"),
        check_vma=False,
    )
```

time: 630 us -> 230 us (0.37)
  local copies, waits for them, and re-layouts: 241 us -> 0.66 us
  other arithmetic: 229 us -> 0.01 us
  Pallas kernels: 0 us -> 106 us
  waiting for transfers between devices: 97.6 us -> 50.2 us
  blocking collectives: 22.7 us -> 58.5 us
  matrix products: 13.4 us -> 1.71 us
  starting transfers between devices: 20.3 us -> 12 us
    scatter-add x2 -> x0, other arithmetic: 177 us -> none  [the longest x1 91.3 us: per_device(): slot_rows = jnp.zeros((peer_count * groups * slot_count, harm_rows), jnp....]
    gather x2 -> x0, local copies, waits for them, and re-layouts: 116 us -> none  [the longest x1 57.9 us: per_device(): jnp.take(arrived_rows, flat_index, axis=0).T.reshape(harm_rows, 4, tr_dev)]
    pallas_call x0 -> x3, Pallas kernels: none -> 106 us  [the longest x1 41.8 us: per_device(): pl.pallas_call(lambda *refs: residual_kernel(rows, slots, *refs), out_sha...]
    all_to_all x2 -> x1, waiting for transfers between devices: 97.6 us -> 50.2 us  [per_device(): lax.all_to_all(outgoing.reshape(peers, half, lanes), ('node', 'freq'), 0,...]
    all_to_all x6 -> x0, local copies, waits for them, and re-layouts: 39.5 us -> none  [the longest x3 17.7 us: per_device(): lax.all_to_all(term_volts, 'freq', split_axis=2, concat_axis=0, tiled=True)]
    reshape x4 -> x0, local copies, waits for them, and re-layouts: 38.6 us -> none  [the longest x1 18.6 us: per_device(): jnp.take(arrived_rows, flat_index, axis=0).T.reshape(harm_rows, 4, tr_dev)]
    all_to_all x2 -> x1, blocking collectives: 22.7 us -> 58.5 us  [per_device(): lax.all_to_all(returned.reshape(peers, half, lanes), ('node', 'freq'), 0,...]
    unnamed x17 -> x8, local copies, waits for them, and re-layouts: 30.5 us -> 0.64 us
  transfers between devices with their start and end apart: 2 -> 1, of which waited for: 2 -> 1; matrix products, arithmetic and copies ran while one was open for 1% -> 1% of each run, Pallas kernels for 0% -> 0%
where the time goes in v1:
time: 230 us; the launch traced here: 229 us
  Pallas kernels  106 us (46%)
  blocking collectives  58.5 us (25%)
  waiting for transfers between devices  50.2 us (22%)
  starting transfers between devices  12 us (5%)
    all_to_all x1, blocking collectives, per_device(): lax.all_to_all(returned.reshape(peers, half, lanes), ('node', 'freq'), 0,...  58.5 us
    all_to_all x1, waiting for transfers between devices, per_device(): lax.all_to_all(outgoing.reshape(peers, half, lanes), ('node', 'freq'), 0,...  50.2 us
    pallas_call x1, Pallas kernels, per_device(): pl.pallas_call(lambda *refs: residual_kernel(rows, slots, *refs), out_sha...  41.8 us
    pallas_call x1, Pallas kernels, per_device(): pl.pallas_call(device_kernel, out_shape=jax.ShapeDtypeStruct((senders, 2,...  34.2 us
    pallas_call x1, Pallas kernels, per_device(): pl.pallas_call(lambda *refs: pick_kernel(rows, slots, *refs), out_shape=j...  30.3 us
    all_to_all x1, starting transfers between devices, per_device(): lax.all_to_all(outgoing.reshape(peers, half, lanes), ('node', 'freq'), 0,...  12 us
  transfers between devices with their start and end apart: 1, of which 1 were waited for; matrix products, arithmetic and copies ran while one was open for 1% of the time, Pallas kernels for 0%

profile of v1, /device:TPU:1, one launch (start us, length us, event | category | flops | bytes accessed | tf_op | source)
XLA Modules:
  0.0 229.5 jit_solution(18243664733483214213)
XLA Ops:
  0.0 0.0 copy-start
  0.0 30.3 %pick.1 = f32[8192,128]{1,0:T(8,128)} custom-call(s32[16384]{0:T(1024)} %bitcast.12, f32[64,16384]{1,0:T(8,128)} %refs_3_.1), custom_call_target="tpu_custom_call" | custom-call | tf_op jit(solution)/shard_map/pick/pallas_call | solution.py:304
  30.4 0.0 copy-start.1
  30.4 0.0 copy-start.2
  30.4 0.0 slice-start
  30.4 12.0 %all-to-all-start = ((f32[128,64,128]{2,1,0:T(8,128)}), f32[128,64,128]{2,1,0:T(8,128)}, u32[]{:S(2)}, u32[]{:S(2)}) async-start(f32[128,64,128]{2,1,0:T(8,128)} %bitcast.10), calls=%async_computation | async-start | bytes 8388608 | tf_op jit(solution)/shard_map/all_to_all | solution.py:320
  42.4 0.0 copy-done.1
  42.4 0.0 copy-done.2
  42.4 0.0 copy-done
  42.5 0.6 copy.13
  43.1 0.0 slice-done
  43.1 1.7 fusion.params
  44.8 50.2 %all-to-all-done = f32[128,64,128]{2,1,0:T(8,128)} async-done(((f32[128,64,128]{2,1,0:T(8,128)}), f32[128,64,128]{2,1,0:T(8,128)}, u32[]{:S(2)}, u32[]{:S(2)}) %all-to-all-start) | async-done | bytes 4194336 | tf_op jit(solution)/shard_map/all_to_all | solution.py:320
  95.0 34.2 %devices.1 = f32[64,2,64,128]{3,2,1,0:T(8,128)} custom-call(s32[8192]{0:T(1024)} %bitcast.14, f32[2048,6]{1,0:T(8,128)} %fusion.params, bf16[256,256]{1,0:T(8,128)(2,1)} %constant.20.clone.syn_hi, bf16[256,256]{1,0:T(8,128)(2,1)} %constant.21.clone.syn_lo, bf16[256,512]{1,0:T(8,128)(2,1)} %constant.22.clone.ana_hi, bf16[256,512]{1,0:T(8,128)(2,1)} %constant.23.clone.ana_lo, ...), custom_call_target="tpu_custom_call" | custom-call | tf_op jit(solution)/shard_map/devices/pallas_call | solution.py:343
  129.2 58.5 %all_to_all.10 = f32[128,64,128]{2,1,0:T(8,128)} all-to-all(f32[128,64,128]{2,1,0:T(8,128)} %bitcast.11), channel_id=1, replica_groups=mesh['node'=64,'freq'=2] {'node','freq'}, dimensions={0} | all-to-all | bytes 8388608 | tf_op jit(solution)/shard_map/all_to_all | solution.py:361
  187.7 41.8 %residual.1 = f32[64,16384]{1,0:T(8,128)} custom-call(s32[16384]{0:T(1024)} %bitcast.13, f32[1,16384]{1,0:T(1,128)} %bitcast.15, f32[8192,128]{1,0:T(8,128)} %bitcast.9, f32[64,16384]{1,0:T(8,128)} %refs_3_.1), custom_call_target="tpu_custom_call" | custom-call | tf_op jit(solution)/shard_map/residual/pallas_call | solution.py:363
  (4 shorter events, 0.0 us)
Async XLA Ops:
  0.0 42.4 %copy-start = (s32[4,4096]{1,0:T(4,128)S(1)}, s32[4,4096]{1,0:T(4,128)}, u32[]{:S(2)}) copy-start(s32[4,4096]{1,0:T(4,128)} %param.15) | copy-start | bytes 196612
  30.4 12.0 %copy-start.1 = (f32[6,64]{1,0:T(8,128)S(1)}, f32[6,64]{1,0:T(8,128)}, u32[]{:S(2)}) copy-start(f32[6,64]{1,0:T(8,128)} %param.12) | copy-start | bytes 4612
  30.4 12.0 %copy-start.2 = (s32[4096]{0:T(1024)S(1)}, s32[4096]{0:T(1024)}, u32[]{:S(2)}) copy-start(s32[4096]{0:T(1024)} %param.13) | copy-start | bytes 49156
  30.4 12.7 %slice-start = ((f32[6,64]{1,0:T(8,128)}), f32[2,64]{1,0:T(2,128)S(1)}, s32[]{:S(2)}) async-start(f32[6,64]{1,0:T(8,128)} %param.12), calls=%async_computation.2 | async-start | bytes 2048 | tf_op jit(solution)/shard_map/slice | solution.py:325
  30.4 64.6 %all-to-all-start = ((f32[128,64,128]{2,1,0:T(8,128)}), f32[128,64,128]{2,1,0:T(8,128)}, u32[]{:S(2)}, u32[]{:S(2)}) async-start(f32[128,64,128]{2,1,0:T(8,128)} %bitcast.10), calls=%async_computation | async-start | bytes 8388608 | tf_op jit(solution)/shard_map/all_to_all | solution.py:320

commit v2 on v1

--- a/solution.py
+++ b/solution.py
@@ -10,6 +10,8 @@
 HIGH = lax.Precision.HIGHEST
 F32 = jnp.float32
 BF16 = jnp.bfloat16
+BATCH = 16
+TEAM = 8
 
 
 def dft_tables(npoints):
@@ -50,7 +52,7 @@
     return jnp.maximum(x, 0.0) + jnp.log1p(jnp.exp(-jnp.abs(x)))
 
 
-def pick_kernel(rows, slots, idx, v_hbm, out_hbm, vbuf, table, obuf, in_sem, out_sem):
+def pick_kernel(rows, slots, idx_hbm, v_hbm, out_hbm, idx, vbuf, table, obuf, idx_sem, in_sem, out_sem):
     nodes = vbuf.shape[1]
     n_in = in_sem.shape[0]
     n_out = out_sem.shape[0]
@@ -69,40 +71,53 @@
 
     for c in range(n_in):
         fetch(c).start()
+    idx_copy = pltpu.make_async_copy(idx_hbm, idx, idx_sem)
+    idx_copy.start()
     table[pl.ds(nodes, 8), :] = jnp.zeros((8, 128), F32)
+    low = lax.broadcasted_iota(jnp.int32, (128, 128), 1) < rows
     for c in range(n_in):
         fetch(c).wait()
 
         def turn(b, carry, c=c):
-            at = pl.multiple_of(c * width + b * 128, 128)
-            x = vbuf[:, pl.ds(at, 128)]
-            table[pl.ds(at, 128), :] = jnp.concatenate([x, x], axis=0).T
-            return carry
-
-        lax.fori_loop(0, width // 128, turn, 0)
-    low = lax.broadcasted_iota(jnp.int32, (1, 128), 1) < rows
-
-    def group(c, carry):
-        def peer(q, carry):
-            p = c * per_out + q
-            for j in range(half):
-                a = idx[p * slots + j]
-                b = idx[p * slots + half + j]
-                obuf[pl.ds(p * half + j, 1), :] = jnp.where(low, table[pl.ds(a, 1), :], table[pl.ds(b, 1), :])
-            return carry
-
-        lax.fori_loop(0, per_out, peer, 0)
+            for w in range(2):
+                at = pl.multiple_of(c * width + (b * 2 + w) * 256, 256)
+                x = jnp.concatenate([vbuf[:, pl.ds(at, 128)], vbuf[:, pl.ds(at + 128, 128)]], axis=0).T
+                y = pltpu.roll(x, rows, 1)
+                table[pl.ds(at, 128), :] = jnp.where(low, x, y)
+                table[pl.ds(at + 128, 128), :] = jnp.where(low, y, x)
+            return carry
+
+        lax.fori_loop(0, width // 512, turn, 0)
+    idx_copy.wait()
+
+    for c in range(n_out):
+
+        def rounds(i, carry, c=c):
+            for w in range(4):
+                j = i * 4 + w
+                for p in range(c * per_out, (c + 1) * per_out):
+                    a = table[pl.ds(idx.at[pl.ds(p * slots, half)][j], 1), :]
+                    b = table[pl.ds(idx.at[pl.ds(p * slots + half, half)][j], 1), :]
+                    obuf.at[pl.ds(p * half, half)][pl.ds(j, 1), :] = jnp.where(low[:1], a, b)
+            return carry
+
+        lax.fori_loop(0, half // 4, rounds, 0)
         ship(c).start()
-        return carry
-
-    lax.fori_loop(0, n_out, group, 0)
     for c in range(n_out):
         ship(c).wait()
 
 
+def add_rows(table, names, rows):
+    spots = [pl.ds(name, 1) for name in names]
+    sums = [table[spot, :] + row for spot, row in zip(spots, rows)]
+    for spot, total in zip(spots, sums):
+        table[spot, :] = total
+
+
 def device_kernel(
-    idx, params, syn_hi, syn_lo, ana_hi, ana_lo, x_hbm, out_hbm,
-    xbuf, wave, gbuf, qbuf, abuf, acc0, acc1, acc2, acc3, in_sem, out_sem,
+    idx_hbm, first_hbm, flags_hbm, params_hbm, syn_hi_hbm, syn_lo_hbm, ana_hi_hbm, ana_lo_hbm, x_hbm, out_hbm,
+    idx, first, flags, params, syn_hi, syn_lo, ana_hi, ana_lo,
+    xbuf, wave, gbuf, qbuf, abuf, acc0, acc1, acc2, acc3, own_sem, in_sem, out_sem,
 ):
     accs = (acc0, acc1, acc2, acc3)
     senders, _, half, lanes = xbuf.shape
@@ -112,6 +127,7 @@
     per_out = senders // n_out
     tr_local = params.shape[0]
     chunk = gbuf.shape[1]
+    batches = tr_local // BATCH
     sub = 64
 
     def fetch(c):
@@ -122,15 +138,31 @@
         part = pl.ds(c * per_out, per_out)
         return pltpu.make_async_copy(xbuf.at[part], out_hbm.at[part], out_sem.at[c])
 
+    own = [
+        pltpu.make_async_copy(source, copy, own_sem.at[i])
+        for i, (source, copy) in enumerate(
+            [
+                (syn_hi_hbm, syn_hi), (syn_lo_hbm, syn_lo), (idx_hbm, idx), (params_hbm, params),
+                (ana_hi_hbm, ana_hi), (ana_lo_hbm, ana_lo), (first_hbm, first), (flags_hbm, flags),
+            ]
+        )
+    ]
+    for copy in own[:2]:
+        copy.start()
     for c in range(n_in):
         fetch(c).start()
+    for copy in own[2:]:
+        copy.start()
 
     def clear(i, carry):
         for acc in accs:
             acc[pl.ds(pl.multiple_of(i * 256, 256), 256), :] = jnp.zeros((256, lanes), F32)
         return carry
 
-    lax.fori_loop(0, acc0.shape[0] // 256, clear, 0)
+    lax.fori_loop(0, wave.shape[0] // 256, clear, 0)
+
+    for copy in own[:2]:
+        copy.wait()
 
     def synth(c, carry):
         fetch(c).wait()
@@ -146,18 +178,22 @@
         return carry
 
     lax.fori_loop(0, n_in, synth, 0)
+    for copy in own[2:]:
+        copy.wait()
 
     def block(c, carry):
         base = c * chunk
 
         def collect(i, carry):
-            t = i * 16
-            for u in range(16):
-                for k in range(4):
-                    gbuf[k, pl.ds(t + u, 1), :] = wave[pl.ds(idx[k * tr_local + base + t + u], 1), :]
-            return carry
-
-        lax.fori_loop(0, chunk // 16, collect, 0)
+            b = c * (chunk // BATCH) + i
+            t = pl.multiple_of(i * BATCH, BATCH)
+            for k in range(4):
+                block = gbuf.at[k, pl.ds(t, BATCH)]
+                for u in range(BATCH):
+                    block[u : u + 1, :] = wave[pl.ds(idx.at[pl.ds((k * BATCH + u) * batches, batches)][b], 1), :]
+            return carry
+
+        lax.fori_loop(0, chunk // BATCH, collect, 0)
 
         def model(i, carry):
             at = pl.ds(pl.multiple_of(i * sub, sub), sub)
@@ -184,14 +220,34 @@
         abuf[3] = -db
 
         def spread(i, carry):
-            t = i * 8
-            for u in range(8):
+            b = c * (chunk // BATCH) + i
+            t = pl.multiple_of(i * BATCH, BATCH)
+            for team in range(0, BATCH, TEAM):
                 for k in range(4):
-                    row = pl.ds(idx[k * tr_local + base + t + u], 1)
-                    accs[k][row, :] = accs[k][row, :] + abuf[k, pl.ds(t + u, 1), :]
-            return carry
-
-        lax.fori_loop(0, chunk // 8, spread, 0)
+                    block = abuf.at[k, pl.ds(t, BATCH)]
+                    add_rows(
+                        accs[k],
+                        [first.at[pl.ds((k * BATCH + u) * batches, batches)][b] for u in range(team, team + TEAM)],
+                        [block[u : u + 1, :] for u in range(team, team + TEAM)],
+                    )
+            return carry
+
+        lax.fori_loop(0, chunk // BATCH, spread, 0)
+
+        def repeat(i, carry):
+            b = c * (chunk // BATCH) + i
+
+            @pl.when(flags[b] != 0)
+            def _():
+                for u in range(BATCH):
+                    for k in range(4):
+                        at = (k * BATCH + u) * batches + b
+                        spot = pl.ds(jnp.where(first[at] == wave.shape[0], idx[at], wave.shape[0]), 1)
+                        accs[k][spot, :] = accs[k][spot, :] + abuf[k, pl.ds(i * BATCH + u, 1), :]
+
+            return carry
+
+        lax.fori_loop(0, chunk // BATCH, repeat, 0)
         return carry
 
     lax.fori_loop(0, tr_local // chunk, block, 0)
@@ -214,8 +270,8 @@
 
 
 def residual_kernel(
-    rows, slots, idx, cond, x_hbm, v_hbm, out_hbm,
-    xbuf, vbuf, low0, low1, high0, high1, in_sem, v_sem, out_sem,
+    rows, slots, idx_hbm, first_hbm, flags_hbm, cond, x_hbm, v_hbm, out_hbm,
+    idx, first, flags, xbuf, vbuf, low0, low1, high0, high1, own_sem, in_sem, v_sem, out_sem,
 ):
     nodes = vbuf.shape[1]
     half = slots // 2
@@ -234,7 +290,14 @@
         return pltpu.make_async_copy(vbuf.at[:, cols], out_hbm.at[:, cols], out_sem.at[c])
 
     v_copy = pltpu.make_async_copy(v_hbm, vbuf, v_sem)
-    for c in range(n_in):
+    own = [
+        pltpu.make_async_copy(source, copy, own_sem.at[i])
+        for i, (source, copy) in enumerate([(first_hbm, first), (flags_hbm, flags), (idx_hbm, idx)])
+    ]
+    fetch(0).start()
+    for copy in own:
+        copy.start()
+    for c in range(1, n_in):
         fetch(c).start()
     v_copy.start()
 
@@ -245,37 +308,64 @@
 
     lax.fori_loop(0, nodes // 256, clear, 0)
 
-    def group(c, carry):
+    tables = ((low0, high0), (low1, high1))
+    for copy in own:
+        copy.wait()
+
+    for c in range(n_in):
         fetch(c).wait()
-
-        def peer(q, carry):
-            p = c * per_in + q
-            for j in range(half):
-                acc_a, acc_b = ((low0, high0), (low1, high1))[j % 2]
-                x = xbuf[pl.ds(p * half + j, 1), :]
-                a = pl.ds(idx[p * slots + j], 1)
-                b = pl.ds(idx[p * slots + half + j], 1)
-                acc_a[a, :] = acc_a[a, :] + x
-                acc_b[b, :] = acc_b[b, :] + x
-            return carry
-
-        lax.fori_loop(0, per_in, peer, 0)
-        return carry
-
-    lax.fori_loop(0, n_in, group, 0)
+        mine = range(c * per_in, (c + 1) * per_in)
+
+        def slot_pair(i, carry, mine=mine):
+            for team in range(0, BATCH, TEAM):
+                for w in range(2):
+                    for h in range(2):
+                        team_of = mine[team : team + TEAM]
+                        add_rows(
+                            tables[w][h],
+                            [first.at[pl.ds(p * slots + h * half, half)][i * 2 + w] for p in team_of],
+                            [xbuf.at[pl.ds(p * half, half)][pl.ds(i * 2 + w, 1), :] for p in team_of],
+                        )
+            return carry
+
+        lax.fori_loop(0, half // 2, slot_pair, 0)
+
+        def repeat(i, carry, c=c, mine=mine):
+            @pl.when(flags[c * (half // 2) + i] != 0)
+            def _():
+                for w in range(2):
+
+                    def one(q, carry):
+                        p = c * per_in + q
+                        x = xbuf[pl.ds(p * half + i * 2 + w, 1), :]
+                        for h in range(2):
+                            at = p * slots + h * half + i * 2 + w
+                            spot = pl.ds(jnp.where(first[at] == nodes, idx[at], nodes), 1)
+                            tables[w][h][spot, :] = tables[w][h][spot, :] + x
+                        return carry
+
+                    lax.fori_loop(0, BATCH, one, 0)
+
+            return carry
+
+        lax.fori_loop(0, half // 2, repeat, 0)
     v_copy.wait()
     low = lax.broadcasted_iota(jnp.int32, (128, 128), 1) < rows
 
     def finish(c, carry):
         def turn(b, carry):
-            at = pl.multiple_of(c * width + b * 128, 128)
-            part = pl.ds(at, 128)
-            both = jnp.where(low, low0[part, :] + low1[part, :], high0[part, :] + high1[part, :]).T
-            cols = pl.ds(at, 128)
-            vbuf[:, cols] = vbuf[:, cols] * cond[:, cols] + (both[:rows] + both[rows:])
-            return carry
-
-        lax.fori_loop(0, width // 128, turn, 0)
+            for w in range(2):
+                at = pl.multiple_of(c * width + (b * 2 + w) * 256, 256)
+                one, two = pl.ds(at, 128), pl.ds(at + 128, 128)
+                one_low, one_high = low0[one, :] + low1[one, :], high0[one, :] + high1[one, :]
+                two_low, two_high = low0[two, :] + low1[two, :], high0[two, :] + high1[two, :]
+                both = jnp.where(low, one_low, two_high) + pltpu.roll(jnp.where(low, two_low, one_high), rows, 1)
+                both = both.T
+                vbuf[:, one] = vbuf[:, one] * cond[:, one] + both[:rows]
+                vbuf[:, two] = vbuf[:, two] * cond[:, two] + both[rows:]
+            return carry
+
+        lax.fori_loop(0, width // 512, turn, 0)
         ship(c).start()
         return carry
 
@@ -284,7 +374,18 @@
         ship(c).wait()
 
 
-SMEM = pl.BlockSpec(memory_space=pltpu.SMEM)
+def split_repeats(names, axis, spare):
+    columns = [lax.index_in_dim(names, i, axis, keepdims=False) for i in range(names.shape[axis])]
+    seen = [jnp.zeros(columns[0].shape, jnp.bool_)]
+    for i in range(1, len(columns)):
+        hit = columns[i] == columns[0]
+        for j in range(1, i):
+            hit = hit | (columns[i] == columns[j])
+        seen.append(hit)
+    seen = jnp.stack(seen, axis) & (names != spare)
+    return jnp.where(seen, spare, names), seen
+
+
 VMEM = pl.BlockSpec(memory_space=pltpu.VMEM)
 ANY = pl.BlockSpec(memory_space=pl.ANY)
 ROOM = pltpu.CompilerParams(vmem_limit_bytes=60 * 2**20)
@@ -304,12 +405,14 @@
     outgoing = pl.pallas_call(
         lambda *refs: pick_kernel(rows, slots, *refs),
         out_shape=jax.ShapeDtypeStruct((peers * half, lanes), F32),
-        in_specs=[SMEM, ANY],
+        in_specs=[ANY, ANY],
         out_specs=ANY,
         scratch_shapes=[
+            pltpu.SMEM((peers * slots,), jnp.int32),
             pltpu.VMEM((rows, nodes), F32),
             pltpu.VMEM((nodes + 8, lanes), F32),
             pltpu.VMEM((peers * half, lanes), F32),
+            pltpu.SemaphoreType.DMA,
             pltpu.SemaphoreType.DMA((8,)),
             pltpu.SemaphoreType.DMA((8,)),
         ],
@@ -321,7 +424,19 @@
 
     start = lax.axis_index("freq") * tr_local
     index = lax.dynamic_slice_in_dim(model_index, start, tr_local)
-    slot_list = lax.dynamic_slice_in_dim(term_slot, start, tr_local, axis=1).reshape(-1)
+    slot_grid = lax.dynamic_slice_in_dim(term_slot, start, tr_local, axis=1)
+    batches = tr_local // BATCH
+    index = index.reshape(BATCH, batches).T.reshape(-1)
+    slot_list = slot_grid.reshape(-1)
+    slot_grid = slot_grid.reshape(4 * BATCH // TEAM, TEAM, batches)
+    tr_first, tr_seen = split_repeats(slot_grid, 1, senders * slots)
+    tr_first = tr_first.reshape(-1)
+    tr_flags = jnp.any(tr_seen, axis=(0, 1)).astype(jnp.int32)
+    send_grid = send_list.reshape(peers // TEAM, TEAM, slots)
+    send_first, send_seen = split_repeats(send_grid, 1, nodes)
+    send_first = send_first.reshape(-1)
+    send_flags = jnp.any(send_seen.reshape(peers // BATCH, BATCH, 2, half // 2, 2), axis=(1, 2, 4))
+    send_flags = send_flags.astype(jnp.int32).reshape(-1)
     cards = jnp.concatenate([model_table[:2], 1.0 / (1.0 + model_table[2:3]), model_table[3:]], axis=0)
     onehot = (index[:, None] == jnp.arange(cards.shape[1], dtype=jnp.int32)[None, :]).astype(F32)
     params = jnp.dot(onehot, cards.T, precision=HIGH)
@@ -343,34 +458,42 @@
     returned = pl.pallas_call(
         device_kernel,
         out_shape=jax.ShapeDtypeStruct((senders, 2, half, lanes), F32),
-        in_specs=[SMEM, VMEM, VMEM, VMEM, VMEM, VMEM, ANY],
+        in_specs=[ANY] * 9,
         out_specs=ANY,
-        scratch_shapes=[
+        scratch_shapes=[pltpu.SMEM(a.shape, a.dtype) for a in (slot_list, tr_first, tr_flags)]
+        + [pltpu.VMEM(a.shape, a.dtype) for a in (params, syn_hi, syn_lo, ana_hi, ana_lo)]
+        + [
             pltpu.VMEM((senders, 2, half, lanes), F32),
             pltpu.VMEM((senders * slots, lanes), F32),
             pltpu.VMEM((4, chunk, lanes), F32),
             pltpu.VMEM((chunk, 4 * lanes), F32),
             pltpu.VMEM((4, chunk, lanes), F32),
         ]
-        + [pltpu.VMEM((senders * slots, lanes), F32)] * 4
-        + [pltpu.SemaphoreType.DMA((8,)), pltpu.SemaphoreType.DMA((8,))],
+        + [pltpu.VMEM((senders * slots + 8, lanes), F32)] * 4
+        + [pltpu.SemaphoreType.DMA((8,))] * 3,
         compiler_params=ROOM,
         name="devices",
-    )(slot_list, params, syn_hi, syn_lo, ana_hi, ana_lo, arrived.reshape(senders, 2, half, lanes))
+    )(slot_list, tr_first, tr_flags, params, syn_hi, syn_lo, ana_hi, ana_lo, arrived.reshape(senders, 2, half, lanes))
 
     incoming = lax.all_to_all(returned.reshape(peers, half, lanes), ("node", "freq"), 0, 0, tiled=True)
 
     return pl.pallas_call(
         lambda *refs: residual_kernel(rows, slots, *refs),
         out_shape=jax.ShapeDtypeStruct((rows, nodes), F32),
-        in_specs=[SMEM, VMEM, ANY, ANY],
+        in_specs=[ANY, ANY, ANY, VMEM, ANY, ANY],
         out_specs=ANY,
-        scratch_shapes=[pltpu.VMEM((peers * half, lanes), F32), pltpu.VMEM((rows, nodes), F32)]
+        scratch_shapes=[pltpu.SMEM(a.shape, a.dtype) for a in (send_list, send_first, send_flags)]
+        + [pltpu.VMEM((peers * half, lanes), F32), pltpu.VMEM((rows, nodes), F32)]
         + [pltpu.VMEM((nodes + 8, lanes), F32)] * 4
-        + [pltpu.SemaphoreType.DMA((8,)), pltpu.SemaphoreType.DMA, pltpu.SemaphoreType.DMA((8,))],
+        + [
+            pltpu.SemaphoreType.DMA((3,)),
+            pltpu.SemaphoreType.DMA((8,)),
+            pltpu.SemaphoreType.DMA,
+            pltpu.SemaphoreType.DMA((8,)),
+        ],
         compiler_params=ROOM,
         name="residual",
-    )(send_list, node_cond.reshape(1, nodes), incoming.reshape(peers * half, lanes), voltage)
+    )(send_list, send_first, send_flags, node_cond.reshape(1, nodes), incoming.reshape(peers * half, lanes), voltage)
 
 
 def solution(mesh):

time: 230 us -> 197 us (0.86)
  blocking collectives: 58.5 us -> 0 us
  waiting for transfers between devices: 50.2 us -> 99.4 us
  Pallas kernels: 106 us -> 72.6 us
  starting transfers between devices: 12 us -> 17.6 us
  other arithmetic: 0.01 us -> 2.5 us
    all_to_all x1 -> x0, blocking collectives: 58.5 us -> none  [per_device(): lax.all_to_all(returned.reshape(peers, half, lanes), ('node', 'freq'), 0,...]
    all_to_all x0 -> x1, waiting for transfers between devices: none -> 50.2 us  [per_device(): lax.all_to_all(returned.reshape(peers, half, lanes), ('node', 'freq'), 0,...]
    pallas_call x1, Pallas kernels: 41.8 us -> 28 us  [per_device(): pl.pallas_call(lambda *refs: residual_kernel(rows, slots, *refs), out_sha...]
    pallas_call x1, Pallas kernels: 30.3 us -> 17.1 us  [per_device(): pl.pallas_call(lambda *refs: pick_kernel(rows, slots, *refs), out_shape=j...]
    pallas_call x1, Pallas kernels: 34.2 us -> 27.4 us  [per_device(): pl.pallas_call(device_kernel, out_shape=jax.ShapeDtypeStruct((senders, 2,...]
    all_to_all x0 -> x1, starting transfers between devices: none -> 5.63 us  [per_device(): lax.all_to_all(returned.reshape(peers, half, lanes), ('node', 'freq'), 0,...]
  transfers between devices with their start and end apart: 1 -> 2, of which waited for: 1 -> 2; matrix products, arithmetic and copies ran while one was open for 1% -> 3% of each run, Pallas kernels for 0% -> 0%
where the time goes in v2:
time: 197 us; the launch traced here: 196 us
  waiting for transfers between devices  99.4 us (50%)
  Pallas kernels  72.6 us (37%)
  starting transfers between devices  17.6 us (9%)
  other arithmetic  2.5 us (1%)
    all_to_all x1, waiting for transfers between devices, per_device(): lax.all_to_all(returned.reshape(peers, half, lanes), ('node', 'freq'), 0,...  50.2 us
    all_to_all x1, waiting for transfers between devices, per_device(): lax.all_to_all(outgoing.reshape(peers, half, lanes), ('node', 'freq'), 0,...  49.2 us
    pallas_call x1, Pallas kernels, per_device(): pl.pallas_call(lambda *refs: residual_kernel(rows, slots, *refs), out_sha...  28 us
    pallas_call x1, Pallas kernels, per_device(): pl.pallas_call(device_kernel, out_shape=jax.ShapeDtypeStruct((senders, 2,...  27.4 us
    pallas_call x1, Pallas kernels, per_device(): pl.pallas_call(lambda *refs: pick_kernel(rows, slots, *refs), out_shape=j...  17.1 us
    all_to_all x1, starting transfers between devices, per_device(): lax.all_to_all(outgoing.reshape(peers, half, lanes), ('node', 'freq'), 0,...  12 us
    all_to_all x1, starting transfers between devices, per_device(): lax.all_to_all(returned.reshape(peers, half, lanes), ('node', 'freq'), 0,...  5.63 us
  transfers between devices with their start and end apart: 2, of which 2 were waited for; matrix products, arithmetic and copies ran while one was open for 3% of the time, Pallas kernels for 0%

profile of v2, /device:TPU:1, one launch (start us, length us, event | category | flops | bytes accessed | tf_op | source)
XLA Modules:
  0.0 195.7 jit_solution(13350585387842318863)
XLA Ops:
  0.0 17.1 %pick.1 = f32[8192,128]{1,0:T(8,128)} custom-call(s32[16384]{0:T(1024)} %bitcast.25, f32[64,16384]{1,0:T(8,128)} %refs_5_.1), custom_call_target="tpu_custom_call" | custom-call | tf_op jit(solution)/shard_map/pick/pallas_call | solution.py:405
  17.1 0.0 copy-start.3
  17.2 12.0 %all-to-all-start = ((f32[128,64,128]{2,1,0:T(8,128)}), f32[128,64,128]{2,1,0:T(8,128)}, u32[]{:S(2)}, u32[]{:S(2)}) async-start(f32[128,64,128]{2,1,0:T(8,128)} %bitcast.24), calls=%async_computation | async-start | bytes 8388608 | tf_op jit(solution)/shard_map/all_to_all | solution.py:423
  29.2 0.1 compare_or_fusion.6
  29.4 0.1 stack.13
  29.5 0.5 convert_element_type.13.flags_hbm
  30.0 0.1 copy.18
  30.1 0.1 eq.295
  30.2 0.6 fusion.3.first_hbm
  30.8 1.7 fusion.params_hbm
  32.6 49.2 %all-to-all-done = f32[128,64,128]{2,1,0:T(8,128)} async-done(((f32[128,64,128]{2,1,0:T(8,128)}), f32[128,64,128]{2,1,0:T(8,128)}, u32[]{:S(2)}, u32[]{:S(2)}) %all-to-all-start) | async-done | bytes 4194336 | tf_op jit(solution)/shard_map/all_to_all | solution.py:423
  81.8 27.4 %devices.1 = f32[64,2,64,128]{3,2,1,0:T(8,128)} custom-call(s32[8192]{0:T(1024)} %bitcast.31, s32[8192]{0:T(1024)} %fusion.3.first_hbm, s32[128]{0:T(128)} %convert_element_type.13.flags_hbm, f32[2048,6]{1,0:T(8,128)} %fusion.params_hbm, bf16[256,256]{1,0:T(8,128)(2,1)} %constant.8.clone.syn_hi_hbm, bf16[256,256]{1,0:T(8,128)(2,1)} %constant.9.clone.syn_lo_hbm, ...), custom_call_target="tpu_custom_call" | custom-call | tf_op jit(solution)/shard_map/devices/pallas_call | solution.py:458
  109.2 0.0 copy-start.1
  109.2 5.6 %all-to-all-start.1 = ((f32[128,64,128]{2,1,0:T(8,128)}), f32[128,64,128]{2,1,0:T(8,128)}, u32[]{:S(2)}, u32[]{:S(2)}) async-start(f32[128,64,128]{2,1,0:T(8,128)} %bitcast.23), calls=%async_computation.1 | async-start | bytes 8388608 | tf_op jit(solution)/shard_map/all_to_all | solution.py:478
  114.9 0.1 compare_or_fusion
  115.0 0.1 compare_or_fusion.2
  115.1 0.1 stack.10
  115.2 0.1 and_reduce_fusion
  115.4 0.5 reduce_or.29
  116.0 0.2 reduce_or.36
  116.2 0.6 reshape.54.refs_2_
  116.8 0.6 fusion.2.refs_1_
  117.5 50.2 %all-to-all-done.1 = f32[128,64,128]{2,1,0:T(8,128)} async-done(((f32[128,64,128]{2,1,0:T(8,128)}), f32[128,64,128]{2,1,0:T(8,128)}, u32[]{:S(2)}, u32[]{:S(2)}) %all-to-all-start.1) | async-done | bytes 4194336 | tf_op jit(solution)/shard_map/all_to_all | solution.py:478
  167.6 28.0 %residual.1 = f32[64,16384]{1,0:T(8,128)} custom-call(s32[16384]{0:T(1024)} %bitcast.26, s32[16384]{0:T(1024)} %fusion.2.refs_1_, s32[256]{0:T(256)} %reshape.54.refs_2_, f32[1,16384]{1,0:T(1,128)} %bitcast.32, f32[8192,128]{1,0:T(8,128)} %bitcast.11.refs_4_, f32[64,16384]{1,0:T(8,128)} %refs_5_.1), custom_call_target="tpu_custom_call" | custom-call | tf_op jit(solution)/shard_map/residual/pallas_call | solution.py:480
  (24 shorter events, 0.2 us)
Async XLA Ops:
  0.0 29.2 %copy-start = (s32[4,4096]{1,0:T(4,128)S(1)}, s32[4,4096]{1,0:T(4,128)}, u32[]{:S(2)}) copy-start(s32[4,4096]{1,0:T(4,128)} %param.15) | copy-start | bytes 196612
  17.1 12.0 %copy-start.3 = (f32[6,64]{1,0:T(8,128)S(1)}, f32[6,64]{1,0:T(8,128)}, u32[]{:S(2)}) copy-start(f32[6,64]{1,0:T(8,128)} %param.12) | copy-start | bytes 4612
  17.2 12.9 %copy-start.4 = (s32[4096]{0:T(1024)S(1)}, s32[4096]{0:T(1024)}, u32[]{:S(2)}) copy-start(s32[4096]{0:T(1024)} %param.13) | copy-start | bytes 49156
  17.2 13.7 %slice-start = ((f32[6,64]{1,0:T(8,128)}), f32[2,64]{1,0:T(2,128)S(1)}, s32[]{:S(2)}) async-start(f32[6,64]{1,0:T(8,128)} %param.12), calls=%async_computation.2 | async-start | bytes 2048 | tf_op jit(solution)/shard_map/slice | solution.py:440
  17.2 64.6 %all-to-all-start = ((f32[128,64,128]{2,1,0:T(8,128)}), f32[128,64,128]{2,1,0:T(8,128)}, u32[]{:S(2)}, u32[]{:S(2)}) async-start(f32[128,64,128]{2,1,0:T(8,128)} %bitcast.24), calls=%async_computation | async-start | bytes 8388608 | tf_op jit(solution)/shard_map/all_to_all | solution.py:423
  30.0 51.8 %copy-start.2 = (s32[1,16,4,128]{3,1,2,0:T(8,128)}, s32[1,16,4,128]{3,1,2,0:T(8,128)S(1)}, u32[]{:S(2)}) copy-start(s32[1,16,4,128]{3,1,2,0:T(8,128)S(1)} %copy.22) | copy-start | bytes 98308
  109.2 5.6 %copy-start.1 = (s32[1,64,2,128]{3,2,1,0:T(2,128)S(1)}, s32[1,64,2,128]{3,2,1,0:T(2,128)}, u32[]{:S(2)}) copy-start(s32[1,64,2,128]{3,2,1,0:T(2,128)} %param.14) | copy-start | bytes 196612
  109.2 58.4 %all-to-all-start.1 = ((f32[128,64,128]{2,1,0:T(8,128)}), f32[128,64,128]{2,1,0:T(8,128)}, u32[]{:S(2)}, u32[]{:S(2)}) async-start(f32[128,64,128]{2,1,0:T(8,128)} %bitcast.23), calls=%async_computation.1 | async-start | bytes 8388608 | tf_op jit(solution)/shard_map/all_to_all | solution.py:478

commit v3 on v2

v3 whole, which is shorter than its diff:
```python
import jax
import jax.numpy as jnp
import numpy as np
from jax import lax
from jax.experimental import pallas as pl
from jax.experimental.pallas import tpu as pltpu
from jax.sharding import PartitionSpec as P

OMEGA = 0.05
HIGH = lax.Precision.HIGHEST
F32 = jnp.float32
BF16 = jnp.bfloat16
BATCH = 16
TEAM = 4
STEP = 128


def dft_tables(npoints):
    half_len = npoints // 2
    time_idx = np.arange(npoints)[:, None]
    row_idx = np.arange(npoints)[None, :]
    is_sine = (row_idx >= half_len) & (row_idx < npoints - 1)
    edge_row = (row_idx == 0) | (row_idx == npoints - 1)
    harmonic = np.where(row_idx < half_len, row_idx, np.where(row_idx == npoints - 1, half_len, row_idx - half_len + 1))
    phases = 2.0 * np.pi / npoints * (time_idx * harmonic % npoints)
    basis_rows = np.where(is_sine, np.sin(phases), np.cos(phases))
    weight = np.where(edge_row, 1.0 / npoints, 2.0 / npoints)
    deriv_rate = OMEGA * harmonic * weight
    slope_rows = np.where(is_sine, -deriv_rate * np.cos(phases), np.where(edge_row, 0.0, deriv_rate * np.sin(phases)))
    return basis_rows, (weight * basis_rows).T, slope_rows.T


def split_weights(w):
    w = w.astype(np.float32)
    hi = w.astype(jnp.bfloat16)
    lo = (w - hi.astype(np.float32)).astype(jnp.bfloat16)
    return jnp.asarray(np.concatenate([hi, lo, hi], axis=0))


def dot3(x, w3):
    hi = x.astype(BF16)
    lo = (x - hi.astype(F32)).astype(BF16)
    return jnp.dot(jnp.concatenate([hi, hi, lo], axis=1), w3, preferred_element_type=F32)


def soft_bend(values):
    return values + 0.5 * jnp.tanh(values)


def softplus(x):
    return jnp.maximum(x, 0.0) + jnp.log1p(jnp.exp(-jnp.abs(x)))


def pick_kernel(rows, slots, idx_hbm, v_hbm, out_hbm, idx, vbuf, table, obuf, idx_sem, in_sem, out_sem):
    nodes = vbuf.shape[1]
    n_in = in_sem.shape[0]
    n_out = out_sem.shape[0]
    width = nodes // n_in
    half = slots // 2
    peers = obuf.shape[0] // half
    per_out = peers // n_out

    def fetch(c):
        cols = pl.ds(c * width, width)
        return pltpu.make_async_copy(v_hbm.at[:, cols], vbuf.at[:, cols], in_sem.at[c])

    def ship(c):
        part = pl.ds(c * per_out * half, per_out * half)
        return pltpu.make_async_copy(obuf.at[part], out_hbm.at[part], out_sem.at[c])

    for c in range(n_in):
        fetch(c).start()
    idx_copy = pltpu.make_async_copy(idx_hbm, idx, idx_sem)
    idx_copy.start()
    table[pl.ds(nodes, 8), :] = jnp.zeros((8, 128), F32)
    low = lax.broadcasted_iota(jnp.int32, (128, 128), 1) < rows
    for c in range(n_in):
        fetch(c).wait()

        def turn(b, carry, c=c):
            for w in range(8):
                at = pl.multiple_of(c * width + (b * 8 + w) * 256, 256)
                x = jnp.concatenate([vbuf[:, pl.ds(at, 128)], vbuf[:, pl.ds(at + 128, 128)]], axis=0).T
                y = pltpu.roll(x, rows, 1)
                table[pl.ds(at, 128), :] = jnp.where(low, x, y)
                table[pl.ds(at + 128, 128), :] = jnp.where(low, y, x)
            return carry

        lax.fori_loop(0, width // 2048, turn, 0)
    idx_copy.wait()

    for c in range(n_out):

        def rounds(i, carry, c=c):
            for w in range(8):
                j = i * 8 + w
                for p in range(c * per_out, (c + 1) * per_out):
                    a = table[pl.ds(idx.at[pl.ds(p * slots, half)][j], 1), :]
                    b = table[pl.ds(idx.at[pl.ds(p * slots + half, half)][j], 1), :]
                    obuf.at[pl.ds(p * half, half)][pl.ds(j, 1), :] = jnp.where(low[:1], a, b)
            return carry

        lax.fori_loop(0, half // 8, rounds, 0)
        ship(c).start()
    for c in range(n_out):
        ship(c).wait()


def add_rows(table, names, rows):
    spots = [pl.ds(name, 1) for name in names]
    sums = [table[spot, :] + row for spot, row in zip(spots, rows)]
    for spot, total in zip(spots, sums):
        table[spot, :] = total


def device_kernel(
    idx_hbm, first_hbm, flags_hbm, params_hbm, syn_hbm, ana_hbm, x_hbm, out_hbm,
    idx, first, flags, params, syn, ana,
    xbuf, wave, volts0, volts1, duo0, duo1, amps0, amps1, acc0, acc1, acc2, acc3, own_sem, in_sem, out_sem,
):
    accs = (acc0, acc1, acc2, acc3)
    volts, duos, amps = (volts0, volts1), (duo0, duo1), (amps0, amps1)
    senders, _, half, lanes = xbuf.shape
    n_in = in_sem.shape[0]
    n_out = out_sem.shape[0]
    per_in = senders // n_in
    per_out = senders // n_out
    tr_local = params.shape[0]
    batches = tr_local // BATCH
    step = volts0.shape[1]
    inner = step // BATCH
    steps = tr_local // step
    spare = wave.shape[0]

    def fetch(c):
        part = pl.ds(c * per_in, per_in)
        return pltpu.make_async_copy(x_hbm.at[part], xbuf.at[part], in_sem.at[c])

    def ship(c):
        part = pl.ds(c * per_out, per_out)
        return pltpu.make_async_copy(xbuf.at[part], out_hbm.at[part], out_sem.at[c])

    own = [
        pltpu.make_async_copy(source, copy, own_sem.at[i])
        for i, (source, copy) in enumerate(
            [
                (syn_hbm, syn), (idx_hbm, idx), (params_hbm, params),
                (ana_hbm, ana), (first_hbm, first), (flags_hbm, flags),
            ]
        )
    ]
    for copy in own[:1]:
        copy.start()
    for c in range(n_in):
        fetch(c).start()
    for copy in own[1:]:
        copy.start()
    for copy in own[:1]:
        copy.wait()
    rows_in = per_in * 2 * half

    def synth(c, carry):
        at = pl.multiple_of(c * rows_in, rows_in)
        for acc in accs:
            acc[pl.ds(at, rows_in), :] = jnp.zeros((rows_in, lanes), F32)
        fetch(c).wait()
        x = xbuf[pl.ds(c * per_in, per_in)]
        xx = jnp.concatenate(
            [x[:, 0].reshape(per_in * half, lanes), x[:, 1].reshape(per_in * half, lanes)], axis=1
        )
        y = dot3(xx, syn[...])
        for s in range(per_in):
            wave[pl.ds(at + s * 2 * half, half), :] = y[s * half : (s + 1) * half, :lanes]
            wave[pl.ds(at + (s * 2 + 1) * half, half), :] = y[s * half : (s + 1) * half, lanes:]
        return carry

    lax.fori_loop(0, n_in, synth, 0)
    for copy in own[1:]:
        copy.wait()

    def names_of(source, k, b):
        return [source.at[pl.ds((k * BATCH + u) * batches, batches)][b] for u in range(BATCH)]

    def collect(buf, i, q):
        for k in range(4):
            for u, name in enumerate(names_of(idx, k, i * inner + q)):
                buf[k, q * BATCH + u : q * BATCH + u + 1, :] = wave[pl.ds(name, 1), :]

    def model(buf, duo, i, q):
        at = pl.ds(q * BATCH, BATCH)
        par = params[pl.ds(pl.multiple_of(i * step + q * BATCH, BATCH), BATCH), :]
        thresh, strength, inv_slope, cap_gs, cap_gd, cap_db = (par[:, m : m + 1] for m in range(6))
        drain, gate, source, bulk = (buf[k, at, :] for k in range(4))
        pinch = (gate - thresh) * inv_slope
        forward = softplus(0.5 * (pinch - source))
        reverse = softplus(0.5 * (pinch - drain))
        duo[at, 0:lanes] = strength * (forward * forward - reverse * reverse)
        duo[at, lanes : 2 * lanes] = cap_gs * soft_bend(gate - source)
        duo[at, 2 * lanes : 3 * lanes] = cap_gd * soft_bend(gate - drain)
        duo[at, 3 * lanes : 4 * lanes] = cap_db * soft_bend(drain - bulk)

    def analyse(duo, amp):
        left = dot3(duo[:, : 2 * lanes], ana[:, : 2 * lanes])
        right = dot3(duo[:, 2 * lanes :], ana[:, 2 * lanes :])
        chan, gs = left[:, :lanes], left[:, lanes:]
        gd, db = right[:, :lanes], right[:, lanes:]
        amp[0] = chan + (db - gd)
        amp[1] = gs + gd
        amp[2] = -chan - gs
        amp[3] = -db

    def spread(amp, i, q):
        names = [names_of(first, k, i * inner + q) for k in range(4)]
        for team in range(0, BATCH, TEAM):
            for k in range(4):
                at = q * BATCH + team
                add_rows(
                    accs[k],
                    names[k][team : team + TEAM],
                    [amp[k, at + u : at + u + 1, :] for u in range(TEAM)],
                )

    def repeat(amp, i):
        @pl.when(flags[batches + i] != 0)
        def _():
            def batch(q, carry):
                b = i * inner + q

                @pl.when(flags[b] != 0)
                def _():
                    for u in range(BATCH):
                        for k in range(4):
                            at = (k * BATCH + u) * batches + b
                            spot = pl.ds(jnp.where(first[at] == spare, idx[at], spare), 1)
                            accs[k][spot, :] = accs[k][spot, :] + amp[k, pl.ds(q * BATCH + u, 1), :]

                return carry

            lax.fori_loop(0, inner, batch, 0)

    def stage(i, w, *, ahead=None, now=True, before=True, late=None):
        if before:
            analyse(duos[1 - w], amps[1 - w])
        for q in range(inner):
            if ahead is not None:
                collect(volts[1 - w], ahead, q)
            if now:
                model(volts[w], duos[w], i, q)
            if late is not None:
                spread(amps[w], late, q)
        if late is not None:
            repeat(amps[w], late)

    for q in range(inner):
        collect(volts0, 0, q)
    stage(0, 0, ahead=1, before=False)
    stage(1, 1, ahead=2)

    def pair(j, carry):
        for w in range(2):
            i = 2 * j + w
            stage(i, w, ahead=jnp.minimum(i + 1, steps - 1), late=i - 2)
        return carry

    lax.fori_loop(1, steps // 2, pair, 0)
    stage(steps, 0, now=False, late=steps - 2)
    stage(steps + 1, 1, now=False, before=False, late=steps - 1)
    low = lax.broadcasted_iota(jnp.int32, (half, lanes), 1) < half

    def pack(c, carry):
        for s in range(per_out):
            peer = c * per_out + s
            at = pl.multiple_of(peer * 2 * half, 2 * half)
            upper = pl.ds(at + half, half)
            at = pl.ds(at, half)
            one = sum(acc[at, :] for acc in accs)
            two = sum(acc[upper, :] for acc in accs)
            xbuf[peer, 0] = jnp.where(low, one, pltpu.roll(two, half, 1))
            xbuf[peer, 1] = jnp.where(low, pltpu.roll(one, half, 1), two)
        ship(c).start()
        return carry

    lax.fori_loop(0, n_out, pack, 0)
    for c in range(n_out):
        ship(c).wait()


def residual_kernel(
    rows, slots, idx_hbm, first_hbm, flags_hbm, cond_hbm, x_hbm, v_hbm, out_hbm,
    idx, first, flags, cond, xbuf, vbuf, low0, high0, low1, high1, own_sem, in_sem, v_sem, out_sem,
):
    nodes = vbuf.shape[1]
    half = slots // 2
    n_in = in_sem.shape[0]
    n_out = out_sem.shape[0]
    width = nodes // n_out
    peers = xbuf.shape[0] // half
    per_in = peers // n_in

    def fetch(c):
        part = pl.ds(c * per_in * half, per_in * half)
        return pltpu.make_async_copy(x_hbm.at[part], xbuf.at[part], in_sem.at[c])

    def ship(c):
        cols = pl.ds(c * width, width)
        return pltpu.make_async_copy(vbuf.at[:, cols], out_hbm.at[:, cols], out_sem.at[c])

    v_copy = pltpu.make_async_copy(v_hbm, vbuf, v_sem)
    own = [
        pltpu.make_async_copy(source, copy, own_sem.at[i])
        for i, (source, copy) in enumerate([(first_hbm, first), (flags_hbm, flags), (idx_hbm, idx), (cond_hbm, cond)])
    ]
    own[0].start()
    fetch(0).start()
    for copy in own[1:]:
        copy.start()
    for c in range(1, n_in):
        fetch(c).start()
    v_copy.start()

    def clear(i, carry):
        for acc in (low0, high0, low1, high1):
            acc[pl.ds(pl.multiple_of(i * 256, 256), 256), :] = jnp.zeros((256, 128), F32)
        return carry

    lax.fori_loop(0, nodes // 256, clear, 0)

    tables = ((low0, high0), (low1, high1))
    for copy in own:
        copy.wait()

    for c in range(n_in):
        fetch(c).wait()
        mine = range(c * per_in, (c + 1) * per_in)

        def slot_group(i, carry, mine=mine):
            for w in range(8):
                for team in range(0, BATCH, TEAM):
                    for h in range(2):
                        team_of = mine[team : team + TEAM]
                        add_rows(
                            tables[(team // TEAM) % 2][h],
                            [first.at[pl.ds(p * slots + h * half, half)][i * 8 + w] for p in team_of],
                            [xbuf.at[pl.ds(p * half, half)][pl.ds(i * 8 + w, 1), :] for p in team_of],
                        )
            return carry

        lax.fori_loop(0, half // 8, slot_group, 0)

        def repeat(i, carry, c=c, mine=mine):
            @pl.when(flags[c * half + i] != 0)
            def _():
                for q in range(BATCH):
                    x = xbuf[pl.ds(mine[q] * half + i, 1), :]
                    for h in range(2):
                        at = mine[q] * slots + h * half + i
                        spot = pl.ds(jnp.where(first[at] == nodes, idx[at], nodes), 1)
                        tables[0][h][spot, :] = tables[0][h][spot, :] + x

            return carry

        @pl.when(flags[n_in * (half + 8) + c] != 0)
        def _(repeat=repeat, c=c):
            def eighth(e, carry):
                @pl.when(flags[n_in * half + c * 8 + e] != 0)
                def _():
                    lax.fori_loop(0, half // 8, lambda i, z: repeat(e * (half // 8) + i, z), 0)

                return carry

            lax.fori_loop(0, 8, eighth, 0)

    v_copy.wait()
    low = lax.broadcasted_iota(jnp.int32, (128, 128), 1) < rows

    def finish(c, carry):
        def turn(b, carry):
            for w in range(8):
                at = pl.multiple_of(c * width + (b * 8 + w) * 256, 256)
                one, two = pl.ds(at, 128), pl.ds(at + 128, 128)
                both = jnp.where(low, low0[one, :] + low1[one, :], high0[two, :] + high1[two, :])
                both = both + pltpu.roll(jnp.where(low, low0[two, :] + low1[two, :], high0[one, :] + high1[one, :]), rows, 1)
                both = both.T
                vbuf[:, one] = vbuf[:, one] * cond[:, one] + both[:rows]
                vbuf[:, two] = vbuf[:, two] * cond[:, two] + both[rows:]
            return carry

        lax.fori_loop(0, width // 2048, turn, 0)
        ship(c).start()
        return carry

    lax.fori_loop(0, n_out, finish, 0)
    for c in range(n_out):
        ship(c).wait()


def split_repeats(names, axis, spare):
    columns = [lax.index_in_dim(names, i, axis, keepdims=False) for i in range(names.shape[axis])]
    seen = [jnp.zeros(columns[0].shape, jnp.bool_)]
    for i in range(1, len(columns)):
        hit = columns[i] == columns[0]
        for j in range(1, i):
            hit = hit | (columns[i] == columns[j])
        seen.append(hit)
    seen = jnp.stack(seen, axis) & (names != spare)
    return jnp.where(seen, spare, names), seen


ANY = pl.BlockSpec(memory_space=pl.ANY)
ROOM = pltpu.CompilerParams(vmem_limit_bytes=60 * 2**20)


def per_device(voltage, node_cond, model_table, model_index, send_nodes, term_slot):
    rows, nodes = voltage.shape
    senders = send_nodes.shape[1]
    groups = send_nodes.shape[2]
    slots = send_nodes.shape[3]
    half = slots // 2
    peers = senders * groups
    lanes = rows * groups
    tr_local = term_slot.shape[1] // groups
    send_list = send_nodes.reshape(-1)

    outgoing = pl.pallas_call(
        lambda *refs: pick_kernel(rows, slots, *refs),
        out_shape=jax.ShapeDtypeStruct((peers * half, lanes), F32),
        in_specs=[ANY, ANY],
        out_specs=ANY,
        scratch_shapes=[
            pltpu.SMEM((peers * slots,), jnp.int32),
            pltpu.VMEM((rows, nodes), F32),
            pltpu.VMEM((nodes + 8, lanes), F32),
            pltpu.VMEM((peers * half, lanes), F32),
            pltpu.SemaphoreType.DMA,
            pltpu.SemaphoreType.DMA((8,)),
            pltpu.SemaphoreType.DMA((8,)),
        ],
        compiler_params=ROOM,
        name="pick",
    )(send_list, voltage)

    arrived = lax.all_to_all(outgoing.reshape(peers, half, lanes), ("node", "freq"), 0, 0, tiled=True)

    start = lax.axis_index("freq") * tr_local
    index = lax.dynamic_slice_in_dim(model_index, start, tr_local)
    slot_grid = lax.dynamic_slice_in_dim(term_slot, start, tr_local, axis=1)
    batches = tr_local // BATCH
    index = index.reshape(BATCH, batches).T.reshape(-1)
    slot_list = slot_grid.reshape(-1)
    slot_grid = slot_grid.reshape(4 * BATCH // TEAM, TEAM, batches)
    tr_first, tr_seen = split_repeats(slot_grid, 1, senders * slots)
    tr_first = tr_first.reshape(-1)
    tr_flags = jnp.any(tr_seen, axis=(0, 1))
    tr_flags = jnp.concatenate([tr_flags, jnp.any(tr_flags.reshape(-1, STEP // BATCH), axis=1)]).astype(jnp.int32)
    send_grid = send_list.reshape(peers // TEAM, TEAM, slots)
    send_first, send_seen = split_repeats(send_grid, 1, nodes)
    send_first = send_first.reshape(-1)
    send_flags = jnp.any(send_seen.reshape(peers // BATCH, BATCH, 2, half), axis=(1, 2))
    send_flags = jnp.concatenate(
        [
            send_flags.reshape(-1),
            jnp.any(send_flags.reshape(peers // BATCH, 8, half // 8), axis=2).reshape(-1),
            jnp.any(send_flags, axis=1),
        ]
    ).astype(jnp.int32)
    cards = jnp.concatenate([model_table[:2], 1.0 / (1.0 + model_table[2:3]), model_table[3:]], axis=0)
    onehot = (index[:, None] == jnp.arange(cards.shape[1], dtype=jnp.int32)[None, :]).astype(F32)
    params = jnp.dot(onehot, cards.T, precision=HIGH)

    synthesis, analysis, slope_table = dft_tables(lanes)
    syn = np.zeros((2, 2, rows, 2, lanes))
    for f in range(2):
        for q in range(2):
            syn[f, q, :, q, :] = synthesis.T[f * rows : (f + 1) * rows]
    none = np.zeros((lanes, lanes))
    ana = np.concatenate(
        [np.block([[analysis.T, none], [none, slope_table.T]]), np.block([[slope_table.T, none], [none, slope_table.T]])],
        axis=1,
    )
    syn = split_weights(syn.reshape(2 * lanes, 2 * lanes))
    ana = split_weights(ana)

    returned = pl.pallas_call(
        device_kernel,
        out_shape=jax.ShapeDtypeStruct((senders, 2, half, lanes), F32),
        in_specs=[ANY] * 7,
        out_specs=ANY,
        scratch_shapes=[pltpu.SMEM(a.shape, a.dtype) for a in (slot_list, tr_first, tr_flags)]
        + [pltpu.VMEM(a.shape, a.dtype) for a in (params, syn, ana)]
        + [
            pltpu.VMEM((senders, 2, half, lanes), F32),
            pltpu.VMEM((senders * slots, lanes), F32),
        ]
        + [pltpu.VMEM((4, STEP, lanes), F32)] * 2
        + [pltpu.VMEM((STEP, 4 * lanes), F32)] * 2
        + [pltpu.VMEM((4, STEP, lanes), F32)] * 2
        + [pltpu.VMEM((senders * slots + 8, lanes), F32)] * 4
        + [pltpu.SemaphoreType.DMA((8,))] * 3,
        compiler_params=ROOM,
        name="devices",
    )(slot_list, tr_first, tr_flags, params, syn, ana, arrived.reshape(senders, 2, half, lanes))

    incoming = lax.all_to_all(returned.reshape(peers, half, lanes), ("node", "freq"), 0, 0, tiled=True)

    return pl.pallas_call(
        lambda *refs: residual_kernel(rows, slots, *refs),
        out_shape=jax.ShapeDtypeStruct((rows, nodes), F32),
        in_specs=[ANY] * 6,
        out_specs=ANY,
        scratch_shapes=[pltpu.SMEM(a.shape, a.dtype) for a in (send_list, send_first, send_flags)]
        + [pltpu.VMEM((1, nodes), F32), pltpu.VMEM((peers * half, lanes), F32), pltpu.VMEM((rows, nodes), F32)]
        + [pltpu.VMEM((nodes + 8, lanes), F32)] * 4
        + [
            pltpu.SemaphoreType.DMA((4,)),
            pltpu.SemaphoreType.DMA((8,)),
            pltpu.SemaphoreType.DMA,
            pltpu.SemaphoreType.DMA((8,)),
        ],
        compiler_params=ROOM,
        name="residual",
    )(send_list, send_first, send_flags, node_cond.reshape(1, nodes), incoming.reshape(peers * half, lanes), voltage)


def solution(mesh):
    return jax.shard_map(
        per_device,
        mesh=mesh,
        in_specs=(
            P("freq", "node"),
            P("node"),
            P(),
            P("node"),
            P("node", None, None, None),
            P(None, "node"),
        ),
        out_specs=P("freq", "node"),
        check_vma=False,
    )
```

time: 197 us -> 179 us (0.909)
  Pallas kernels: 72.6 us -> 55.2 us
  other arithmetic: 2.5 us -> 4.75 us
    pallas_call x1, Pallas kernels: 28 us -> 18.4 us  [per_device(): pl.pallas_call(lambda *refs: residual_kernel(rows, slots, *refs), out_sha...]
    pallas_call x1, Pallas kernels: 27.4 us -> 22.3 us  [per_device(): pl.pallas_call(device_kernel, out_shape=jax.ShapeDtypeStruct((senders, 2,...]
    pallas_call x1, Pallas kernels: 17.1 us -> 14.4 us  [per_device(): pl.pallas_call(lambda *refs: pick_kernel(rows, slots, *refs), out_shape=j...]
  transfers between devices with their start and end apart: 2 -> 2, of which waited for: 2 -> 2; matrix products, arithmetic and copies ran while one was open for 3% -> 4% of each run, Pallas kernels for 0% -> 0%
where the time goes in v3:
time: 179 us
  waiting for transfers between devices  97.8 us (55%)
  Pallas kernels  55.2 us (31%)
  starting transfers between devices  17.8 us (10%)
  other arithmetic  4.75 us (3%)
    all_to_all x1, waiting for transfers between devices, per_device(): lax.all_to_all(outgoing.reshape(peers, half, lanes), ('node', 'freq'), 0,...  49 us
    all_to_all x1, waiting for transfers between devices, per_device(): lax.all_to_all(returned.reshape(peers, half, lanes), ('node', 'freq'), 0,...  48.8 us
    pallas_call x1, Pallas kernels, per_device(): pl.pallas_call(device_kernel, out_shape=jax.ShapeDtypeStruct((senders, 2,...  22.3 us
    pallas_call x1, Pallas kernels, per_device(): pl.pallas_call(lambda *refs: residual_kernel(rows, slots, *refs), out_sha...  18.4 us
    pallas_call x1, Pallas kernels, per_device(): pl.pallas_call(lambda *refs: pick_kernel(rows, slots, *refs), out_shape=j...  14.4 us
    all_to_all x1, starting transfers between devices, per_device(): lax.all_to_all(outgoing.reshape(peers, half, lanes), ('node', 'freq'), 0,...  12 us
    all_to_all x1, starting transfers between devices, per_device(): lax.all_to_all(returned.reshape(peers, half, lanes), ('node', 'freq'), 0,...  5.87 us
  transfers between devices with their start and end apart: 2, of which 2 were waited for; matrix products, arithmetic and copies ran while one was open for 4% of the time, Pallas kernels for 0%

profile of v3, /device:TPU:1, one launch (start us, length us, event | category | flops | bytes accessed | tf_op | source)
XLA Modules:
  0.0 178.6 jit_solution(15402322324885337219)
XLA Ops:
  0.0 14.4 %pick.1 = f32[8192,128]{1,0:T(8,128)} custom-call(s32[16384]{0:T(1024)} %bitcast.20, f32[64,16384]{1,0:T(8,128)} %refs_5_.1), custom_call_target="tpu_custom_call" | custom-call | tf_op jit(solution)/shard_map/pick/pallas_call | solution.py:424
  14.4 12.0 %all-to-all-start = ((f32[128,64,128]{2,1,0:T(8,128)}), f32[128,64,128]{2,1,0:T(8,128)}, u32[]{:S(2)}, u32[]{:S(2)}) async-start(f32[128,64,128]{2,1,0:T(8,128)} %bitcast.18), calls=%async_computation | async-start | bytes 8388608 | tf_op jit(solution)/shard_map/all_to_all | solution.py:442
  26.6 0.1 and_reduce_fusion
  26.7 0.1 reshape.64
  26.8 0.1 reduce_or.85
  27.0 0.1 copy.13
  27.2 0.5 add_convert_fusion.1.flags_hbm
  27.7 0.6 and_select_fusion.1.first_hbm
  28.3 1.7 fusion.params_hbm
  30.0 49.0 %all-to-all-done = f32[128,64,128]{2,1,0:T(8,128)} async-done(((f32[128,64,128]{2,1,0:T(8,128)}), f32[128,64,128]{2,1,0:T(8,128)}, u32[]{:S(2)}, u32[]{:S(2)}) %all-to-all-start) | async-done | bytes 4194336 | tf_op jit(solution)/shard_map/all_to_all | solution.py:442
  79.1 22.3 %devices.1 = f32[64,2,64,128]{3,2,1,0:T(8,128)} custom-call(s32[8192]{0:T(1024)} %bitcast.25, s32[8192]{0:T(1024)} %and_select_fusion.1.first_hbm, s32[144]{0:T(256)} %add_convert_fusion.1.flags_hbm, f32[2048,6]{1,0:T(8,128)} %fusion.params_hbm, bf16[768,256]{1,0:T(8,128)(2,1)} %constant.6.clone.syn_hbm, bf16[768,512]{1,0:T(8,128)(2,1)} %constant.7.clone.ana_hbm, ...), custom_call_target="tpu_custom_call" | custom-call | tf_op jit(solution)/shard_map/devices/pallas_call | solution.py:483
  101.4 5.9 %all-to-all-start.1 = ((f32[128,64,128]{2,1,0:T(8,128)}), f32[128,64,128]{2,1,0:T(8,128)}, u32[]{:S(2)}, u32[]{:S(2)}) async-start(f32[128,64,128]{2,1,0:T(8,128)} %bitcast.19), calls=%async_computation.1 | async-start | bytes 8388608 | tf_op jit(solution)/shard_map/all_to_all | solution.py:503
  107.3 0.1 slice_compare_fusion
  107.4 0.1 pad_add_fusion
  107.5 1.2 fusion.8
  109.1 0.2 reduce_or.62
  109.4 0.1 reshape.60
  109.4 0.1 reduce_or.80
  109.6 0.1 reduce_or.81
  109.8 0.1 reduce_or.83
  109.9 0.7 add_convert_fusion.refs_2_
  110.6 0.6 and_select_fusion.refs_1_
  111.2 48.8 %all-to-all-done.1 = f32[128,64,128]{2,1,0:T(8,128)} async-done(((f32[128,64,128]{2,1,0:T(8,128)}), f32[128,64,128]{2,1,0:T(8,128)}, u32[]{:S(2)}, u32[]{:S(2)}) %all-to-all-start.1) | async-done | bytes 4194336 | tf_op jit(solution)/shard_map/all_to_all | solution.py:503
  160.1 18.4 %residual.1 = f32[64,16384]{1,0:T(8,128)} custom-call(s32[16384]{0:T(1024)} %bitcast.21, s32[16384]{0:T(1024)} %and_select_fusion.refs_1_, s32[584]{0:T(1024)} %add_convert_fusion.refs_2_, f32[1,16384]{1,0:T(1,128)} %bitcast.27, f32[8192,128]{1,0:T(8,128)} %bitcast.10.refs_4_, f32[64,16384]{1,0:T(8,128)} %refs_5_.1), custom_call_target="tpu_custom_call" | custom-call | tf_op jit(solution)/shard_map/residual/pallas_call | solution.py:505
  (30 shorter events, 0.7 us)
Async XLA Ops:
  0.0 26.4 %copy-start = (s32[4,4096]{1,0:T(4,128)S(1)}, s32[4,4096]{1,0:T(4,128)}, u32[]{:S(2)}) copy-start(s32[4,4096]{1,0:T(4,128)} %param.13) | copy-start | bytes 196612
  14.4 12.0 %copy-start.3 = (f32[6,64]{1,0:T(8,128)S(1)}, f32[6,64]{1,0:T(8,128)}, u32[]{:S(2)}) copy-start(f32[6,64]{1,0:T(8,128)} %param.10) | copy-start | bytes 4612
  14.4 12.5 %copy-start.4 = (s32[4096]{0:T(1024)S(1)}, s32[4096]{0:T(1024)}, u32[]{:S(2)}) copy-start(s32[4096]{0:T(1024)} %param.11) | copy-start | bytes 49156
  14.4 13.9 %slice-start = ((f32[6,64]{1,0:T(8,128)}), f32[2,64]{1,0:T(2,128)S(1)}, s32[]{:S(2)}) async-start(f32[6,64]{1,0:T(8,128)} %param.10), calls=%async_computation.2 | async-start | bytes 2048 | tf_op jit(solution)/shard_map/slice | solution.py:466
  14.4 64.6 %all-to-all-start = ((f32[128,64,128]{2,1,0:T(8,128)}), f32[128,64,128]{2,1,0:T(8,128)}, u32[]{:S(2)}, u32[]{:S(2)}) async-start(f32[128,64,128]{2,1,0:T(8,128)} %bitcast.18), calls=%async_computation | async-start | bytes 8388608 | tf_op jit(solution)/shard_map/all_to_all | solution.py:442
  27.0 52.1 %copy-start.2 = (s32[1,16,4,128]{3,1,2,0:T(8,128)}, s32[1,16,4,128]{3,1,2,0:T(8,128)S(1)}, u32[]{:S(2)}) copy-start(s32[1,16,4,128]{3,1,2,0:T(8,128)S(1)} %copy.16) | copy-start | bytes 98308
  101.4 5.9 %copy-start.1 = (s32[1,64,2,128]{3,2,1,0:T(2,128)S(1)}, s32[1,64,2,128]{3,2,1,0:T(2,128)}, u32[]{:S(2)}) copy-start(s32[1,64,2,128]{3,2,1,0:T(2,128)} %param.12) | copy-start | bytes 196612
  101.4 58.6 %all-to-all-start.1 = ((f32[128,64,128]{2,1,0:T(8,128)}), f32[128,64,128]{2,1,0:T(8,128)}, u32[]{:S(2)}, u32[]{:S(2)}) async-start(f32[128,64,128]{2,1,0:T(8,128)} %bitcast.19), calls=%async_computation.1 | async-start | bytes 8388608 | tf_op jit(solution)/shard_map/all_to_all | solution.py:503

commit v4 on v3

--- a/solution.py
+++ b/solution.py
@@ -168,7 +168,7 @@
         xx = jnp.concatenate(
             [x[:, 0].reshape(per_in * half, lanes), x[:, 1].reshape(per_in * half, lanes)], axis=1
         )
-        y = dot3(xx, syn[...])
+        y = jnp.concatenate([dot3(part, syn[...]) for part in jnp.split(xx, 2, axis=0)], axis=0)
         for s in range(per_in):
             wave[pl.ds(at + s * 2 * half, half), :] = y[s * half : (s + 1) * half, :lanes]
             wave[pl.ds(at + (s * 2 + 1) * half, half), :] = y[s * half : (s + 1) * half, lanes:]
@@ -221,22 +221,17 @@
                 )
 
     def repeat(amp, i):
-        @pl.when(flags[batches + i] != 0)
-        def _():
-            def batch(q, carry):
-                b = i * inner + q
-
-                @pl.when(flags[b] != 0)
-                def _():
-                    for u in range(BATCH):
-                        for k in range(4):
-                            at = (k * BATCH + u) * batches + b
-                            spot = pl.ds(jnp.where(first[at] == spare, idx[at], spare), 1)
-                            accs[k][spot, :] = accs[k][spot, :] + amp[k, pl.ds(q * BATCH + u, 1), :]
-
-                return carry
-
-            lax.fori_loop(0, inner, batch, 0)
+        def batch(n, carry):
+            q = flags[steps + i * inner + n]
+            b = i * inner + q
+            for u in range(BATCH):
+                for k in range(4):
+                    at = (k * BATCH + u) * batches + b
+                    spot = pl.ds(jnp.where(first[at] == spare, idx[at], spare), 1)
+                    accs[k][spot, :] = accs[k][spot, :] + amp[k, pl.ds(q * BATCH + u, 1), :]
+            return carry
+
+        lax.fori_loop(0, flags[i], batch, 0)
 
     def stage(i, w, *, ahead=None, now=True, before=True, late=None):
         if before:
@@ -347,28 +342,18 @@
 
         lax.fori_loop(0, half // 8, slot_group, 0)
 
-        def repeat(i, carry, c=c, mine=mine):
-            @pl.when(flags[c * half + i] != 0)
-            def _():
-                for q in range(BATCH):
-                    x = xbuf[pl.ds(mine[q] * half + i, 1), :]
-                    for h in range(2):
-                        at = mine[q] * slots + h * half + i
-                        spot = pl.ds(jnp.where(first[at] == nodes, idx[at], nodes), 1)
-                        tables[0][h][spot, :] = tables[0][h][spot, :] + x
-
+        def repeat(n, carry, c=c, mine=mine):
+            i = flags[n_in + c * half + n]
+            for q in range(BATCH):
+                x = xbuf[pl.ds(mine[q] * half + i, 1), :]
+                for h in range(2):
+                    at = mine[q] * slots + h * half + i
+                    spot = pl.ds(jnp.where(first[at] == nodes, idx[at], nodes), 1)
+                    table = tables[q % 2][h]
+                    table[spot, :] = table[spot, :] + x
             return carry
 
-        @pl.when(flags[n_in * (half + 8) + c] != 0)
-        def _(repeat=repeat, c=c):
-            def eighth(e, carry):
-                @pl.when(flags[n_in * half + c * 8 + e] != 0)
-                def _():
-                    lax.fori_loop(0, half // 8, lambda i, z: repeat(e * (half // 8) + i, z), 0)
-
-                return carry
-
-            lax.fori_loop(0, 8, eighth, 0)
+        lax.fori_loop(0, flags[c], repeat, 0)
 
     v_copy.wait()
     low = lax.broadcasted_iota(jnp.int32, (128, 128), 1) < rows
@@ -404,6 +389,15 @@
         seen.append(hit)
     seen = jnp.stack(seen, axis) & (names != spare)
     return jnp.where(seen, spare, names), seen
+
+
+def marked(flags):
+    n = flags.shape[1]
+    place = jnp.arange(n, dtype=jnp.int32)
+    rank = jnp.sum((flags[:, None, :] & (place[None, None, :] < place[None, :, None])).astype(jnp.int32), axis=2)
+    hit = flags[:, None, :] & (rank[:, None, :] == place[None, :, None])
+    order = jnp.sum(jnp.where(hit, place[None, None, :], 0), axis=2)
+    return jnp.concatenate([jnp.sum(flags.astype(jnp.int32), axis=1), order.reshape(-1)])
 
 
 ANY = pl.BlockSpec(memory_space=pl.ANY)
@@ -450,19 +444,12 @@
     slot_grid = slot_grid.reshape(4 * BATCH // TEAM, TEAM, batches)
     tr_first, tr_seen = split_repeats(slot_grid, 1, senders * slots)
     tr_first = tr_first.reshape(-1)
-    tr_flags = jnp.any(tr_seen, axis=(0, 1))
-    tr_flags = jnp.concatenate([tr_flags, jnp.any(tr_flags.reshape(-1, STEP // BATCH), axis=1)]).astype(jnp.int32)
+    tr_flags = marked(jnp.any(tr_seen, axis=(0, 1)).reshape(-1, STEP // BATCH))
     send_grid = send_list.reshape(peers // TEAM, TEAM, slots)
     send_first, send_seen = split_repeats(send_grid, 1, nodes)
     send_first = send_first.reshape(-1)
     send_flags = jnp.any(send_seen.reshape(peers // BATCH, BATCH, 2, half), axis=(1, 2))
-    send_flags = jnp.concatenate(
-        [
-            send_flags.reshape(-1),
-            jnp.any(send_flags.reshape(peers // BATCH, 8, half // 8), axis=2).reshape(-1),
-            jnp.any(send_flags, axis=1),
-        ]
-    ).astype(jnp.int32)
+    send_flags = marked(send_flags)
     cards = jnp.concatenate([model_table[:2], 1.0 / (1.0 + model_table[2:3]), model_table[3:]], axis=0)
     onehot = (index[:, None] == jnp.arange(cards.shape[1], dtype=jnp.int32)[None, :]).astype(F32)
     params = jnp.dot(onehot, cards.T, precision=HIGH)

time: 179 us -> 178 us (level)
  no operation moved by 1% of the time
where the time goes in v4:
time: 178 us
  waiting for transfers between devices  98.8 us (56%)
  Pallas kernels  55.2 us (31%)
  starting transfers between devices  17.4 us (10%)
  other arithmetic  3.92 us (2%)
    all_to_all x1, waiting for transfers between devices, per_device(): lax.all_to_all(returned.reshape(peers, half, lanes), ('node', 'freq'), 0,...  50.2 us
    all_to_all x1, waiting for transfers between devices, per_device(): lax.all_to_all(outgoing.reshape(peers, half, lanes), ('node', 'freq'), 0,...  48.6 us
    pallas_call x1, Pallas kernels, per_device(): pl.pallas_call(device_kernel, out_shape=jax.ShapeDtypeStruct((senders, 2,...  22.6 us
    pallas_call x1, Pallas kernels, per_device(): pl.pallas_call(lambda *refs: residual_kernel(rows, slots, *refs), out_sha...  18.2 us
    pallas_call x1, Pallas kernels, per_device(): pl.pallas_call(lambda *refs: pick_kernel(rows, slots, *refs), out_shape=j...  14.4 us
    all_to_all x1, starting transfers between devices, per_device(): lax.all_to_all(outgoing.reshape(peers, half, lanes), ('node', 'freq'), 0,...  12 us
    all_to_all x1, starting transfers between devices, per_device(): lax.all_to_all(returned.reshape(peers, half, lanes), ('node', 'freq'), 0,...  5.4 us
  transfers between devices with their start and end apart: 2, of which 2 were waited for; matrix products, arithmetic and copies ran while one was open for 4% of the time, Pallas kernels for 0%

profile of v4, /device:TPU:1, one launch (start us, length us, event | category | flops | bytes accessed | tf_op | source)
XLA Modules:
  0.0 178.2 jit_solution(6850177268701048528)
XLA Ops:
  0.0 14.4 %pick.1 = f32[8192,128]{1,0:T(8,128)} custom-call(s32[16384]{0:T(1024)} %bitcast.20, f32[64,16384]{1,0:T(8,128)} %refs_5_.1), custom_call_target="tpu_custom_call" | custom-call | tf_op jit(solution)/shard_map/pick/pallas_call | solution.py:418
  14.4 12.0 %all-to-all-start = ((f32[128,64,128]{2,1,0:T(8,128)}), f32[128,64,128]{2,1,0:T(8,128)}, u32[]{:S(2)}, u32[]{:S(2)}) async-start(f32[128,64,128]{2,1,0:T(8,128)} %bitcast.18), calls=%async_computation | async-start | bytes 8388608 | tf_op jit(solution)/shard_map/all_to_all | solution.py:436
  26.6 0.1 and_reduce_fusion.1
  26.7 0.1 reshape.89
  26.9 0.1 convert_reduce_fusion.1
  27.1 0.1 reshape.90
  27.2 0.1 copy.15
  27.4 0.1 convert_reduce_fusion.2
  27.5 0.6 pad_add_fusion.3.flags_hbm
  28.2 0.6 and_select_fusion.1.first_hbm
  28.8 1.7 fusion.params_hbm
  30.5 48.6 %all-to-all-done = f32[128,64,128]{2,1,0:T(8,128)} async-done(((f32[128,64,128]{2,1,0:T(8,128)}), f32[128,64,128]{2,1,0:T(8,128)}, u32[]{:S(2)}, u32[]{:S(2)}) %all-to-all-start) | async-done | bytes 4194336 | tf_op jit(solution)/shard_map/all_to_all | solution.py:436
  79.1 22.6 %devices.1 = f32[64,2,64,128]{3,2,1,0:T(8,128)} custom-call(s32[8192]{0:T(1024)} %bitcast.25, s32[8192]{0:T(1024)} %and_select_fusion.1.first_hbm, s32[144]{0:T(256)} %pad_add_fusion.3.flags_hbm, f32[2048,6]{1,0:T(8,128)} %fusion.params_hbm, bf16[768,256]{1,0:T(8,128)(2,1)} %constant.6.clone.syn_hbm, bf16[768,512]{1,0:T(8,128)(2,1)} %constant.7.clone.ana_hbm, ...), custom_call_target="tpu_custom_call" | custom-call | tf_op jit(solution)/shard_map/devices/pallas_call | solution.py:470
  101.7 5.4 %all-to-all-start.1 = ((f32[128,64,128]{2,1,0:T(8,128)}), f32[128,64,128]{2,1,0:T(8,128)}, u32[]{:S(2)}, u32[]{:S(2)}) async-start(f32[128,64,128]{2,1,0:T(8,128)} %bitcast.19), calls=%async_computation.1 | async-start | bytes 8388608 | tf_op jit(solution)/shard_map/all_to_all | solution.py:490
  107.1 0.1 slice_compare_fusion
  107.2 0.1 pad_add_fusion
  107.3 0.1 and_reduce_fusion
  107.6 0.2 convert_reduce_fusion
  107.9 0.2 select_reduce_fusion
  108.2 0.1 convert_reduce_fusion.3
  108.3 0.7 pad_add_fusion.2.refs_2_
  108.9 0.6 and_select_fusion.refs_1_
  109.6 50.2 %all-to-all-done.1 = f32[128,64,128]{2,1,0:T(8,128)} async-done(((f32[128,64,128]{2,1,0:T(8,128)}), f32[128,64,128]{2,1,0:T(8,128)}, u32[]{:S(2)}, u32[]{:S(2)}) %all-to-all-start.1) | async-done | bytes 4194336 | tf_op jit(solution)/shard_map/all_to_all | solution.py:490
  159.8 18.2 %residual.1 = f32[64,16384]{1,0:T(8,128)} custom-call(s32[16384]{0:T(1024)} %bitcast.21, s32[16384]{0:T(1024)} %and_select_fusion.refs_1_, s32[520]{0:T(1024)} %pad_add_fusion.2.refs_2_, f32[1,16384]{1,0:T(1,128)} %bitcast.27, f32[8192,128]{1,0:T(8,128)} %bitcast.10.refs_4_, f32[64,16384]{1,0:T(8,128)} %refs_5_.1), custom_call_target="tpu_custom_call" | custom-call | tf_op jit(solution)/shard_map/residual/pallas_call | solution.py:492
  (33 shorter events, 0.7 us)
Async XLA Ops:
  0.0 26.4 %copy-start = (s32[4,4096]{1,0:T(4,128)S(1)}, s32[4,4096]{1,0:T(4,128)}, u32[]{:S(2)}) copy-start(s32[4,4096]{1,0:T(4,128)} %param.13) | copy-start | bytes 196612
  14.4 12.0 %copy-start.3 = (f32[6,64]{1,0:T(8,128)S(1)}, f32[6,64]{1,0:T(8,128)}, u32[]{:S(2)}) copy-start(f32[6,64]{1,0:T(8,128)} %param.10) | copy-start | bytes 4612
  14.4 12.8 %copy-start.4 = (s32[4096]{0:T(1024)S(1)}, s32[4096]{0:T(1024)}, u32[]{:S(2)}) copy-start(s32[4096]{0:T(1024)} %param.11) | copy-start | bytes 49156
  14.4 14.4 %slice-start = ((f32[6,64]{1,0:T(8,128)}), f32[2,64]{1,0:T(2,128)S(1)}, s32[]{:S(2)}) async-start(f32[6,64]{1,0:T(8,128)} %param.10), calls=%async_computation.2 | async-start | bytes 2048 | tf_op jit(solution)/shard_map/slice | solution.py:453
  14.4 64.6 %all-to-all-start = ((f32[128,64,128]{2,1,0:T(8,128)}), f32[128,64,128]{2,1,0:T(8,128)}, u32[]{:S(2)}, u32[]{:S(2)}) async-start(f32[128,64,128]{2,1,0:T(8,128)} %bitcast.18), calls=%async_computation | async-start | bytes 8388608 | tf_op jit(solution)/shard_map/all_to_all | solution.py:436
  27.2 51.8 %copy-start.2 = (s32[1,16,4,128]{3,1,2,0:T(8,128)}, s32[1,16,4,128]{3,1,2,0:T(8,128)S(1)}, u32[]{:S(2)}) copy-start(s32[1,16,4,128]{3,1,2,0:T(8,128)S(1)} %copy.18) | copy-start | bytes 98308
  101.6 5.4 %copy-start.1 = (s32[1,64,2,128]{3,2,1,0:T(2,128)S(1)}, s32[1,64,2,128]{3,2,1,0:T(2,128)}, u32[]{:S(2)}) copy-start(s32[1,64,2,128]{3,2,1,0:T(2,128)} %param.12) | copy-start | bytes 196612
  101.7 58.2 %all-to-all-start.1 = ((f32[128,64,128]{2,1,0:T(8,128)}), f32[128,64,128]{2,1,0:T(8,128)}, u32[]{:S(2)}, u32[]{:S(2)}) async-start(f32[128,64,128]{2,1,0:T(8,128)} %bitcast.19), calls=%async_computation.1 | async-start | bytes 8388608 | tf_op jit(solution)/shard_map/all_to_all | solution.py:490

commit v5 on v4

--- a/solution.py
+++ b/solution.py
@@ -74,34 +74,38 @@
     idx_copy.start()
     table[pl.ds(nodes, 8), :] = jnp.zeros((8, 128), F32)
     low = lax.broadcasted_iota(jnp.int32, (128, 128), 1) < rows
-    for c in range(n_in):
+    def turn(c, carry):
         fetch(c).wait()
-
-        def turn(b, carry, c=c):
-            for w in range(8):
-                at = pl.multiple_of(c * width + (b * 8 + w) * 256, 256)
-                x = jnp.concatenate([vbuf[:, pl.ds(at, 128)], vbuf[:, pl.ds(at + 128, 128)]], axis=0).T
-                y = pltpu.roll(x, rows, 1)
-                table[pl.ds(at, 128), :] = jnp.where(low, x, y)
-                table[pl.ds(at + 128, 128), :] = jnp.where(low, y, x)
+        for w in range(width // 256):
+            at = pl.multiple_of(c * width + w * 256, 256)
+            x = jnp.concatenate([vbuf[:, pl.ds(at, 128)], vbuf[:, pl.ds(at + 128, 128)]], axis=0).T
+            y = pltpu.roll(x, rows, 1)
+            table[pl.ds(at, 128), :] = jnp.where(low, x, y)
+            table[pl.ds(at + 128, 128), :] = jnp.where(low, y, x)
+        return carry
+
+    lax.fori_loop(0, n_in, turn, 0)
+    idx_copy.wait()
+
+    def tail(ref, offset):
+        return ref.at[pl.ds(offset, ref.shape[0] - offset)]
+
+    def group(c, carry):
+        def rounds(i, carry):
+            for w in range(16):
+                j = i * 16 + w
+                name, out = c * (per_out * slots) + j, c * (per_out * half) + j
+                for p in range(per_out):
+                    a = table[pl.ds(tail(idx, p * slots)[name], 1), :]
+                    b = table[pl.ds(tail(idx, p * slots + half)[name], 1), :]
+                    tail(obuf, p * half)[pl.ds(out, 1), :] = jnp.where(low[:1], a, b)
             return carry
 
-        lax.fori_loop(0, width // 2048, turn, 0)
-    idx_copy.wait()
-
-    for c in range(n_out):
-
-        def rounds(i, carry, c=c):
-            for w in range(8):
-                j = i * 8 + w
-                for p in range(c * per_out, (c + 1) * per_out):
-                    a = table[pl.ds(idx.at[pl.ds(p * slots, half)][j], 1), :]
-                    b = table[pl.ds(idx.at[pl.ds(p * slots + half, half)][j], 1), :]
-                    obuf.at[pl.ds(p * half, half)][pl.ds(j, 1), :] = jnp.where(low[:1], a, b)
-            return carry
-
-        lax.fori_loop(0, half // 8, rounds, 0)
+        lax.fori_loop(0, half // 16, rounds, 0)
         ship(c).start()
+        return carry
+
+    lax.fori_loop(0, n_out, group, 0)
     for c in range(n_out):
         ship(c).wait()
 
@@ -324,37 +328,43 @@
     for copy in own:
         copy.wait()
 
-    for c in range(n_in):
+    def tail(ref, offset):
+        return ref.at[pl.ds(offset, ref.shape[0] - offset)]
+
+    def group(c, carry):
         fetch(c).wait()
-        mine = range(c * per_in, (c + 1) * per_in)
-
-        def slot_group(i, carry, mine=mine):
-            for w in range(8):
+
+        def slot_group(i, carry):
+            for w in range(16):
+                j = i * 16 + w
+                name, row = c * (per_in * slots) + j, c * (per_in * half) + j
                 for team in range(0, BATCH, TEAM):
                     for h in range(2):
-                        team_of = mine[team : team + TEAM]
                         add_rows(
                             tables[(team // TEAM) % 2][h],
-                            [first.at[pl.ds(p * slots + h * half, half)][i * 8 + w] for p in team_of],
-                            [xbuf.at[pl.ds(p * half, half)][pl.ds(i * 8 + w, 1), :] for p in team_of],
+                            [tail(first, q * slots + h * half)[name] for q in range(team, team + TEAM)],
+                            [tail(xbuf, q * half)[pl.ds(row, 1), :] for q in range(team, team + TEAM)],
                         )
             return carry
 
-        lax.fori_loop(0, half // 8, slot_group, 0)
-
-        def repeat(n, carry, c=c, mine=mine):
+        lax.fori_loop(0, half // 16, slot_group, 0)
+
+        def repeat(n, carry):
             i = flags[n_in + c * half + n]
             for q in range(BATCH):
-                x = xbuf[pl.ds(mine[q] * half + i, 1), :]
+                p = c * per_in + q
+                x = xbuf[pl.ds(p * half + i, 1), :]
                 for h in range(2):
-                    at = mine[q] * slots + h * half + i
+                    at = p * slots + h * half + i
                     spot = pl.ds(jnp.where(first[at] == nodes, idx[at], nodes), 1)
                     table = tables[q % 2][h]
                     table[spot, :] = table[spot, :] + x
             return carry
 
         lax.fori_loop(0, flags[c], repeat, 0)
-
+        return carry
+
+    lax.fori_loop(0, n_in, group, 0)
     v_copy.wait()
     low = lax.broadcasted_iota(jnp.int32, (128, 128), 1) < rows
 

time: 178 us -> 178 us (level)
  no operation moved by 1% of the time
where the time goes in v5:
time: 178 us
  waiting for transfers between devices  98.8 us (56%)
  Pallas kernels  55 us (31%)
  starting transfers between devices  17.6 us (10%)
  other arithmetic  3.92 us (2%)
    all_to_all x1, waiting for transfers between devices, per_device(): lax.all_to_all(returned.reshape(peers, half, lanes), ('node', 'freq'), 0,...  50.2 us
    all_to_all x1, waiting for transfers between devices, per_device(): lax.all_to_all(outgoing.reshape(peers, half, lanes), ('node', 'freq'), 0,...  48.6 us
    pallas_call x1, Pallas kernels, per_device(): pl.pallas_call(device_kernel, out_shape=jax.ShapeDtypeStruct((senders, 2,...  22.3 us
    pallas_call x1, Pallas kernels, per_device(): pl.pallas_call(lambda *refs: residual_kernel(rows, slots, *refs), out_sha...  18.2 us
    pallas_call x1, Pallas kernels, per_device(): pl.pallas_call(lambda *refs: pick_kernel(rows, slots, *refs), out_shape=j...  14.5 us
    all_to_all x1, starting transfers between devices, per_device(): lax.all_to_all(outgoing.reshape(peers, half, lanes), ('node', 'freq'), 0,...  12 us
    all_to_all x1, starting transfers between devices, per_device(): lax.all_to_all(returned.reshape(peers, half, lanes), ('node', 'freq'), 0,...  5.64 us
  transfers between devices with their start and end apart: 2, of which 2 were waited for; matrix products, arithmetic and copies ran while one was open for 4% of the time, Pallas kernels for 0%

profile of v5, /device:TPU:1, one launch (start us, length us, event | category | flops | bytes accessed | tf_op | source)
XLA Modules:
  0.0 178.1 jit_solution(17537104419135233222)
XLA Ops:
  0.0 14.5 %pick.1 = f32[8192,128]{1,0:T(8,128)} custom-call(s32[16384]{0:T(1024)} %bitcast.20, f32[64,16384]{1,0:T(8,128)} %refs_5_.1), custom_call_target="tpu_custom_call" | custom-call | tf_op jit(solution)/shard_map/pick/pallas_call | solution.py:428
  14.6 12.0 %all-to-all-start = ((f32[128,64,128]{2,1,0:T(8,128)}), f32[128,64,128]{2,1,0:T(8,128)}, u32[]{:S(2)}, u32[]{:S(2)}) async-start(f32[128,64,128]{2,1,0:T(8,128)} %bitcast.18), calls=%async_computation | async-start | bytes 8388608 | tf_op jit(solution)/shard_map/all_to_all | solution.py:446
  26.7 0.1 and_reduce_fusion.1
  26.8 0.1 reshape.89
  27.0 0.1 convert_reduce_fusion.1
  27.2 0.1 reshape.90
  27.4 0.1 copy.15
  27.5 0.1 convert_reduce_fusion.2
  27.7 0.6 pad_add_fusion.3.flags_hbm
  28.3 0.6 and_select_fusion.1.first_hbm
  28.9 1.7 fusion.params_hbm
  30.6 48.6 %all-to-all-done = f32[128,64,128]{2,1,0:T(8,128)} async-done(((f32[128,64,128]{2,1,0:T(8,128)}), f32[128,64,128]{2,1,0:T(8,128)}, u32[]{:S(2)}, u32[]{:S(2)}) %all-to-all-start) | async-done | bytes 4194336 | tf_op jit(solution)/shard_map/all_to_all | solution.py:446
  79.2 22.3 %devices.1 = f32[64,2,64,128]{3,2,1,0:T(8,128)} custom-call(s32[8192]{0:T(1024)} %bitcast.25, s32[8192]{0:T(1024)} %and_select_fusion.1.first_hbm, s32[144]{0:T(256)} %pad_add_fusion.3.flags_hbm, f32[2048,6]{1,0:T(8,128)} %fusion.params_hbm, bf16[768,256]{1,0:T(8,128)(2,1)} %constant.6.clone.syn_hbm, bf16[768,512]{1,0:T(8,128)(2,1)} %constant.7.clone.ana_hbm, ...), custom_call_target="tpu_custom_call" | custom-call | tf_op jit(solution)/shard_map/devices/pallas_call | solution.py:480
  101.5 5.6 %all-to-all-start.1 = ((f32[128,64,128]{2,1,0:T(8,128)}), f32[128,64,128]{2,1,0:T(8,128)}, u32[]{:S(2)}, u32[]{:S(2)}) async-start(f32[128,64,128]{2,1,0:T(8,128)} %bitcast.19), calls=%async_computation.1 | async-start | bytes 8388608 | tf_op jit(solution)/shard_map/all_to_all | solution.py:500
  107.2 0.1 slice_compare_fusion
  107.3 0.1 pad_add_fusion
  107.4 0.1 and_reduce_fusion
  107.7 0.2 convert_reduce_fusion
  108.0 0.2 select_reduce_fusion
  108.3 0.1 convert_reduce_fusion.3
  108.4 0.7 pad_add_fusion.2.refs_2_
  109.0 0.6 and_select_fusion.refs_1_
  109.7 50.2 %all-to-all-done.1 = f32[128,64,128]{2,1,0:T(8,128)} async-done(((f32[128,64,128]{2,1,0:T(8,128)}), f32[128,64,128]{2,1,0:T(8,128)}, u32[]{:S(2)}, u32[]{:S(2)}) %all-to-all-start.1) | async-done | bytes 4194336 | tf_op jit(solution)/shard_map/all_to_all | solution.py:500
  159.9 18.2 %residual.1 = f32[64,16384]{1,0:T(8,128)} custom-call(s32[16384]{0:T(1024)} %bitcast.21, s32[16384]{0:T(1024)} %and_select_fusion.refs_1_, s32[520]{0:T(1024)} %pad_add_fusion.2.refs_2_, f32[1,16384]{1,0:T(1,128)} %bitcast.27, f32[8192,128]{1,0:T(8,128)} %bitcast.10.refs_4_, f32[64,16384]{1,0:T(8,128)} %refs_5_.1), custom_call_target="tpu_custom_call" | custom-call | tf_op jit(solution)/shard_map/residual/pallas_call | solution.py:502
  (33 shorter events, 0.7 us)
Async XLA Ops:
  0.0 26.6 %copy-start = (s32[4,4096]{1,0:T(4,128)S(1)}, s32[4,4096]{1,0:T(4,128)}, u32[]{:S(2)}) copy-start(s32[4,4096]{1,0:T(4,128)} %param.13) | copy-start | bytes 196612
  14.5 12.0 %copy-start.3 = (f32[6,64]{1,0:T(8,128)S(1)}, f32[6,64]{1,0:T(8,128)}, u32[]{:S(2)}) copy-start(f32[6,64]{1,0:T(8,128)} %param.10) | copy-start | bytes 4612
  14.5 12.8 %copy-start.4 = (s32[4096]{0:T(1024)S(1)}, s32[4096]{0:T(1024)}, u32[]{:S(2)}) copy-start(s32[4096]{0:T(1024)} %param.11) | copy-start | bytes 49156
  14.6 14.4 %slice-start = ((f32[6,64]{1,0:T(8,128)}), f32[2,64]{1,0:T(2,128)S(1)}, s32[]{:S(2)}) async-start(f32[6,64]{1,0:T(8,128)} %param.10), calls=%async_computation.2 | async-start | bytes 2048 | tf_op jit(solution)/shard_map/slice | solution.py:463
  14.6 64.6 %all-to-all-start = ((f32[128,64,128]{2,1,0:T(8,128)}), f32[128,64,128]{2,1,0:T(8,128)}, u32[]{:S(2)}, u32[]{:S(2)}) async-start(f32[128,64,128]{2,1,0:T(8,128)} %bitcast.18), calls=%async_computation | async-start | bytes 8388608 | tf_op jit(solution)/shard_map/all_to_all | solution.py:446
  27.3 51.8 %copy-start.2 = (s32[1,16,4,128]{3,1,2,0:T(8,128)}, s32[1,16,4,128]{3,1,2,0:T(8,128)S(1)}, u32[]{:S(2)}) copy-start(s32[1,16,4,128]{3,1,2,0:T(8,128)S(1)} %copy.18) | copy-start | bytes 98308
  101.5 5.7 %copy-start.1 = (s32[1,64,2,128]{3,2,1,0:T(2,128)S(1)}, s32[1,64,2,128]{3,2,1,0:T(2,128)}, u32[]{:S(2)}) copy-start(s32[1,64,2,128]{3,2,1,0:T(2,128)} %param.12) | copy-start | bytes 196612
  101.5 58.4 %all-to-all-start.1 = ((f32[128,64,128]{2,1,0:T(8,128)}), f32[128,64,128]{2,1,0:T(8,128)}, u32[]{:S(2)}, u32[]{:S(2)}) async-start(f32[128,64,128]{2,1,0:T(8,128)} %bitcast.19), calls=%async_computation.1 | async-start | bytes 8388608 | tf_op jit(solution)/shard_map/all_to_all | solution.py:500

commit v6 on v5

--- a/solution.py
+++ b/solution.py
@@ -238,9 +238,9 @@
         lax.fori_loop(0, flags[i], batch, 0)
 
     def stage(i, w, *, ahead=None, now=True, before=True, late=None):
-        if before:
-            analyse(duos[1 - w], amps[1 - w])
         for q in range(inner):
+            if before and q == inner // 2:
+                analyse(duos[1 - w], amps[1 - w])
             if ahead is not None:
                 collect(volts[1 - w], ahead, q)
             if now:

time: 178 us -> 178 us (level)
  no operation moved by 1% of the time
where the time goes in v6:
time: 178 us
  waiting for transfers between devices  98.8 us (56%)
  Pallas kernels  54.8 us (31%)
  starting transfers between devices  17.6 us (10%)
  other arithmetic  3.92 us (2%)
    all_to_all x1, waiting for transfers between devices, per_device(): lax.all_to_all(returned.reshape(peers, half, lanes), ('node', 'freq'), 0,...  50.2 us
    all_to_all x1, waiting for transfers between devices, per_device(): lax.all_to_all(outgoing.reshape(peers, half, lanes), ('node', 'freq'), 0,...  48.6 us
    pallas_call x1, Pallas kernels, per_device(): pl.pallas_call(device_kernel, out_shape=jax.ShapeDtypeStruct((senders, 2,...  22.3 us
    pallas_call x1, Pallas kernels, per_device(): pl.pallas_call(lambda *refs: residual_kernel(rows, slots, *refs), out_sha...  18 us
    pallas_call x1, Pallas kernels, per_device(): pl.pallas_call(lambda *refs: pick_kernel(rows, slots, *refs), out_shape=j...  14.5 us
    all_to_all x1, starting transfers between devices, per_device(): lax.all_to_all(outgoing.reshape(peers, half, lanes), ('node', 'freq'), 0,...  12 us
    all_to_all x1, starting transfers between devices, per_device(): lax.all_to_all(returned.reshape(peers, half, lanes), ('node', 'freq'), 0,...  5.64 us
  transfers between devices with their start and end apart: 2, of which 2 were waited for; matrix products, arithmetic and copies ran while one was open for 4% of the time, Pallas kernels for 0%

profile of v6, /device:TPU:1, one launch (start us, length us, event | category | flops | bytes accessed | tf_op | source)
XLA Modules:
  0.0 177.9 jit_solution(4193709239937118310)
XLA Ops:
  0.0 14.5 %pick.1 = f32[8192,128]{1,0:T(8,128)} custom-call(s32[16384]{0:T(1024)} %bitcast.20, f32[64,16384]{1,0:T(8,128)} %refs_5_.1), custom_call_target="tpu_custom_call" | custom-call | tf_op jit(solution)/shard_map/pick/pallas_call | solution.py:428
  14.6 12.0 %all-to-all-start = ((f32[128,64,128]{2,1,0:T(8,128)}), f32[128,64,128]{2,1,0:T(8,128)}, u32[]{:S(2)}, u32[]{:S(2)}) async-start(f32[128,64,128]{2,1,0:T(8,128)} %bitcast.18), calls=%async_computation | async-start | bytes 8388608 | tf_op jit(solution)/shard_map/all_to_all | solution.py:446
  26.7 0.1 and_reduce_fusion.1
  26.8 0.1 reshape.89
  27.0 0.1 convert_reduce_fusion.1
  27.2 0.1 reshape.90
  27.4 0.1 copy.15
  27.5 0.1 convert_reduce_fusion.2
  27.7 0.6 pad_add_fusion.3.flags_hbm
  28.3 0.6 and_select_fusion.1.first_hbm
  28.9 1.7 fusion.params_hbm
  30.6 48.6 %all-to-all-done = f32[128,64,128]{2,1,0:T(8,128)} async-done(((f32[128,64,128]{2,1,0:T(8,128)}), f32[128,64,128]{2,1,0:T(8,128)}, u32[]{:S(2)}, u32[]{:S(2)}) %all-to-all-start) | async-done | bytes 4194336 | tf_op jit(solution)/shard_map/all_to_all | solution.py:446
  79.2 22.3 %devices.1 = f32[64,2,64,128]{3,2,1,0:T(8,128)} custom-call(s32[8192]{0:T(1024)} %bitcast.25, s32[8192]{0:T(1024)} %and_select_fusion.1.first_hbm, s32[144]{0:T(256)} %pad_add_fusion.3.flags_hbm, f32[2048,6]{1,0:T(8,128)} %fusion.params_hbm, bf16[768,256]{1,0:T(8,128)(2,1)} %constant.6.clone.syn_hbm, bf16[768,512]{1,0:T(8,128)(2,1)} %constant.7.clone.ana_hbm, ...), custom_call_target="tpu_custom_call" | custom-call | tf_op jit(solution)/shard_map/devices/pallas_call | solution.py:480
  101.4 5.6 %all-to-all-start.1 = ((f32[128,64,128]{2,1,0:T(8,128)}), f32[128,64,128]{2,1,0:T(8,128)}, u32[]{:S(2)}, u32[]{:S(2)}) async-start(f32[128,64,128]{2,1,0:T(8,128)} %bitcast.19), calls=%async_computation.1 | async-start | bytes 8388608 | tf_op jit(solution)/shard_map/all_to_all | solution.py:500
  107.1 0.1 slice_compare_fusion
  107.2 0.1 pad_add_fusion
  107.3 0.1 and_reduce_fusion
  107.7 0.2 convert_reduce_fusion
  107.9 0.2 select_reduce_fusion
  108.2 0.1 convert_reduce_fusion.3
  108.3 0.7 pad_add_fusion.2.refs_2_
  109.0 0.6 and_select_fusion.refs_1_
  109.6 50.2 %all-to-all-done.1 = f32[128,64,128]{2,1,0:T(8,128)} async-done(((f32[128,64,128]{2,1,0:T(8,128)}), f32[128,64,128]{2,1,0:T(8,128)}, u32[]{:S(2)}, u32[]{:S(2)}) %all-to-all-start.1) | async-done | bytes 4194336 | tf_op jit(solution)/shard_map/all_to_all | solution.py:500
  159.9 18.0 %residual.1 = f32[64,16384]{1,0:T(8,128)} custom-call(s32[16384]{0:T(1024)} %bitcast.21, s32[16384]{0:T(1024)} %and_select_fusion.refs_1_, s32[520]{0:T(1024)} %pad_add_fusion.2.refs_2_, f32[1,16384]{1,0:T(1,128)} %bitcast.27, f32[8192,128]{1,0:T(8,128)} %bitcast.10.refs_4_, f32[64,16384]{1,0:T(8,128)} %refs_5_.1), custom_call_target="tpu_custom_call" | custom-call | tf_op jit(solution)/shard_map/residual/pallas_call | solution.py:502
  (33 shorter events, 0.7 us)
Async XLA Ops:
  0.0 26.6 %copy-start = (s32[4,4096]{1,0:T(4,128)S(1)}, s32[4,4096]{1,0:T(4,128)}, u32[]{:S(2)}) copy-start(s32[4,4096]{1,0:T(4,128)} %param.13) | copy-start | bytes 196612
  14.5 12.0 %copy-start.3 = (f32[6,64]{1,0:T(8,128)S(1)}, f32[6,64]{1,0:T(8,128)}, u32[]{:S(2)}) copy-start(f32[6,64]{1,0:T(8,128)} %param.10) | copy-start | bytes 4612
  14.5 12.8 %copy-start.4 = (s32[4096]{0:T(1024)S(1)}, s32[4096]{0:T(1024)}, u32[]{:S(2)}) copy-start(s32[4096]{0:T(1024)} %param.11) | copy-start | bytes 49156
  14.6 14.4 %slice-start = ((f32[6,64]{1,0:T(8,128)}), f32[2,64]{1,0:T(2,128)S(1)}, s32[]{:S(2)}) async-start(f32[6,64]{1,0:T(8,128)} %param.10), calls=%async_computation.2 | async-start | bytes 2048 | tf_op jit(solution)/shard_map/slice | solution.py:463
  14.6 64.6 %all-to-all-start = ((f32[128,64,128]{2,1,0:T(8,128)}), f32[128,64,128]{2,1,0:T(8,128)}, u32[]{:S(2)}, u32[]{:S(2)}) async-start(f32[128,64,128]{2,1,0:T(8,128)} %bitcast.18), calls=%async_computation | async-start | bytes 8388608 | tf_op jit(solution)/shard_map/all_to_all | solution.py:446
  27.3 51.8 %copy-start.2 = (s32[1,16,4,128]{3,1,2,0:T(8,128)}, s32[1,16,4,128]{3,1,2,0:T(8,128)S(1)}, u32[]{:S(2)}) copy-start(s32[1,16,4,128]{3,1,2,0:T(8,128)S(1)} %copy.18) | copy-start | bytes 98308
  101.4 5.7 %copy-start.1 = (s32[1,64,2,128]{3,2,1,0:T(2,128)S(1)}, s32[1,64,2,128]{3,2,1,0:T(2,128)}, u32[]{:S(2)}) copy-start(s32[1,64,2,128]{3,2,1,0:T(2,128)} %param.12) | copy-start | bytes 196612
  101.4 58.4 %all-to-all-start.1 = ((f32[128,64,128]{2,1,0:T(8,128)}), f32[128,64,128]{2,1,0:T(8,128)}, u32[]{:S(2)}, u32[]{:S(2)}) async-start(f32[128,64,128]{2,1,0:T(8,128)} %bitcast.19), calls=%async_computation.1 | async-start | bytes 8388608 | tf_op jit(solution)/shard_map/all_to_all | solution.py:500
